TPU v7x, 32 devices: a whole 2x2x4 slice. The times are simulated.
32 devices in a mesh: clip: 16 (over z, x, core), seq: 2 (over y).
Axes of the slice: x: 2, y: 2, z: 4, core: 2. Of those that a mesh axis runs over, the one named last changes fastest.
Arguments:
- inputs: bfloat16 [32, 128, 768], P('clip', 'seq'), may hold values from -6 to 6
- micro_live: int32 [32], P('clip'), may hold values from 0 to 1, as said below
- ln1_gain: bfloat16 [768], P(('clip', 'seq')), may hold values from 0.099609375 to 1.8984375
- ln1_shift: bfloat16 [768], P(('clip', 'seq')), may hold values from -3 to 3
- w_q: bfloat16 [768, 768], P(('clip', 'seq')), may hold values from -0.21875 to 0.21875
- b_q: bfloat16 [768], P(('clip', 'seq')), may hold values from -4 to 4
- w_k: bfloat16 [768, 768], P(('clip', 'seq')), may hold values from -0.21875 to 0.21875
- w_v: bfloat16 [768, 768], P(('clip', 'seq')), may hold values from -0.21875 to 0.21875
- b_v: bfloat16 [768], P(('clip', 'seq')), may hold values from -3 to 3
- w_o: bfloat16 [768, 768], P(('clip', 'seq')), may hold values from -0.4375 to 0.4375
- b_o: bfloat16 [768], P(('clip', 'seq')), may hold values from -3 to 3
- ln2_gain: bfloat16 [768], P(('clip', 'seq')), may hold values from 0.099609375 to 1.8984375
- ln2_shift: bfloat16 [768], P(('clip', 'seq')), may hold values from -3 to 3
- w_fc1: bfloat16 [768, 3072], P(('clip', 'seq')), may hold values from -0.21875 to 0.21875
- b_fc1: bfloat16 [3072], P(('clip', 'seq')), may hold values from -3 to 3
- w_fc2: bfloat16 [3072, 768], P(('clip', 'seq')), may hold values from -0.109375 to 0.109375
- b_fc2: bfloat16 [768], P(('clip', 'seq')), may hold values from -3 to 3
- grad_out: bfloat16 [32, 128, 768], P('clip', 'seq'), may hold values from -6 to 6
Outputs:
- out_rows: bfloat16 [32, 128, 768], P('clip', 'seq')
- grad_rows: float32 [32, 128, 768], P('clip', 'seq')
- grad_ln1_gain: float32 [768], P(('clip', 'seq'))
- grad_ln1_shift: float32 [768], P(('clip', 'seq'))
- grad_w_q: float32 [768, 768], P(('clip', 'seq'))
- grad_b_q: float32 [768], P(('clip', 'seq'))
- grad_w_k: float32 [768, 768], P(('clip', 'seq'))
- grad_w_v: float32 [768, 768], P(('clip', 'seq'))
- grad_b_v: float32 [768], P(('clip', 'seq'))
- grad_w_o: float32 [768, 768], P(('clip', 'seq'))
- grad_b_o: float32 [768], P(('clip', 'seq'))
- grad_ln2_gain: float32 [768], P(('clip', 'seq'))
- grad_ln2_shift: float32 [768], P(('clip', 'seq'))
- grad_w_fc1: float32 [768, 3072], P(('clip', 'seq'))
- grad_b_fc1: float32 [3072], P(('clip', 'seq'))
- grad_w_fc2: float32 [3072, 768], P(('clip', 'seq'))
- grad_b_fc2: float32 [768], P(('clip', 'seq'))
Inputs may be any that keep to these rules, and one draw needn't show every extreme that they name: `micro_live`: entry 2 * g + m is 1 where micro-batch slot m of clip group g holds a clip, else 0. Slot 0 of every group holds a clip; in every draw some group has all 2 slots filled.
All inputs are finite; a program needn't handle non-finite values.
Results may differ from a plain program's by a relative error of at most 0.013.
Values may be sent and summed in bfloat16 or wider, within the bound.
No kernel may reach another device: no remote copies, remote signals or barrier semaphores. Data moves between devices by JAX's collectives and lax.ppermute only.
A program may use at most 192 MiB of HBM per device.

v0:
```python
import math

import jax
import jax.numpy as jnp
from jax import lax
from jax.sharding import PartitionSpec as P

HEADS = 12
HD = 64


norm_eps = 1e-05


def layer_norm(values, gain, shift):
    center = values - jnp.mean(values, axis=-1, keepdims=True)
    inv_std = lax.rsqrt(jnp.mean(center * center, axis=-1, keepdims=True) + norm_eps)
    normed = center * inv_std
    return (normed * gain + shift, normed, inv_std)


def norm_back(grad_in, normed, inv_std, gain):
    scaled = grad_in * gain
    inner = (
        scaled
        - jnp.mean(scaled, axis=-1, keepdims=True)
        - normed * jnp.mean(scaled * normed, axis=-1, keepdims=True)
    )
    return inv_std * inner


def gelu_slope(pre):
    return (
        0.5 * (1.0 + lax.erf(pre * 0.7071067811865476))
        + pre * jnp.exp(-0.5 * pre * pre) * 0.3989422804014327
    )


def tdot(left, right):
    return jnp.dot(left, right, preferred_element_type=jnp.float32)


def on_device(
    inputs,
    micro_live,
    ln1_gain,
    ln1_shift,
    w_q,
    b_q,
    w_k,
    w_v,
    b_v,
    w_o,
    b_o,
    ln2_gain,
    ln2_shift,
    w_fc1,
    b_fc1,
    w_fc2,
    b_fc2,
    grad_out,
):
    f32 = jnp.float32
    bf16 = jnp.bfloat16
    scale = 1.0 / math.sqrt(HD)
    params = (
        lax.all_gather(ln1_gain, ("clip", "seq"), axis=0, tiled=True),
        lax.all_gather(ln1_shift, ("clip", "seq"), axis=0, tiled=True),
        lax.all_gather(w_q, ("clip", "seq"), axis=0, tiled=True),
        lax.all_gather(b_q, ("clip", "seq"), axis=0, tiled=True),
        lax.all_gather(w_k, ("clip", "seq"), axis=0, tiled=True),
        lax.all_gather(w_v, ("clip", "seq"), axis=0, tiled=True),
        lax.all_gather(b_v, ("clip", "seq"), axis=0, tiled=True),
        lax.all_gather(w_o, ("clip", "seq"), axis=0, tiled=True),
        lax.all_gather(b_o, ("clip", "seq"), axis=0, tiled=True),
        lax.all_gather(ln2_gain, ("clip", "seq"), axis=0, tiled=True),
        lax.all_gather(ln2_shift, ("clip", "seq"), axis=0, tiled=True),
        lax.all_gather(w_fc1, ("clip", "seq"), axis=0, tiled=True),
        lax.all_gather(b_fc1, ("clip", "seq"), axis=0, tiled=True),
        lax.all_gather(w_fc2, ("clip", "seq"), axis=0, tiled=True),
        lax.all_gather(b_fc2, ("clip", "seq"), axis=0, tiled=True),
    )
    g1, c1, wq, bq, wk, wv, bv, wo, bo, g2, c2, wf1, bf1, wf2, bf2 = params
    slots, count, width = inputs.shape
    total_rows = slots * count
    live = micro_live.astype(f32)[:, None, None]
    x = inputs.astype(f32)
    h1, n1, r1 = layer_norm(x, g1.astype(f32), c1.astype(f32))
    h1b = h1.astype(bf16).reshape(total_rows, width)
    qb = (tdot(h1b, wq) + bq.astype(f32)).astype(bf16).reshape(slots, count, width)
    kb = tdot(h1b, wk).astype(bf16).reshape(slots, count, width)
    vb = (tdot(h1b, wv) + bv.astype(f32)).astype(bf16).reshape(slots, count, width)
    key_all, value_all = (
        lax.all_gather(kb, "seq", axis=1, tiled=True),
        lax.all_gather(vb, "seq", axis=1, tiled=True),
    )
    frames = key_all.shape[1]
    q4 = qb.reshape(slots, count, HEADS, HD)
    k4 = key_all.reshape(slots, frames, HEADS, HD)
    v4 = value_all.reshape(slots, frames, HEADS, HD)
    scores = jnp.einsum("sqhd,skhd->shqk", q4, k4, preferred_element_type=f32) * scale
    peak = jnp.max(scores, axis=-1, keepdims=True)
    lse = peak + jnp.log(jnp.sum(jnp.exp(scores - peak), axis=-1, keepdims=True))
    probs = jnp.exp(scores - lse)
    pb = probs.astype(bf16)
    ctxb = (
        jnp.einsum("shqk,skhd->sqhd", pb, v4, preferred_element_type=f32)
        .reshape(total_rows, width)
        .astype(bf16)
    )
    mid = x + tdot(ctxb, wo).reshape(slots, count, width) + bo.astype(f32)
    h2, n2, r2 = layer_norm(mid, g2.astype(f32), c2.astype(f32))
    h2b = h2.astype(bf16).reshape(total_rows, width)
    pre = tdot(h2b, wf1) + bf1.astype(f32)
    actb = jax.nn.gelu(pre, approximate=False).astype(bf16)
    result = (live * (mid + tdot(actb, wf2).reshape(slots, count, width) + bf2.astype(f32))).astype(
        bf16
    )
    gy = live * grad_out.astype(f32)
    gyb = gy.astype(bf16).reshape(total_rows, width)
    dpre = tdot(gyb, wf2.T) * gelu_slope(pre)
    dpreb = dpre.astype(bf16)
    dh2 = tdot(dpreb, wf1.T).reshape(slots, count, width)
    dmid = gy + norm_back(dh2, n2, r2, g2.astype(f32))
    dmidb = dmid.astype(bf16).reshape(total_rows, width)
    dctxb = tdot(dmidb, wo.T).astype(bf16).reshape(slots, count, width)
    dc4 = dctxb.reshape(slots, count, HEADS, HD)
    dprob = jnp.einsum("sqhd,skhd->shqk", dc4, v4, preferred_element_type=f32)
    delta = jnp.sum(probs * dprob, axis=-1, keepdims=True)
    dsb = (probs * (dprob - delta) * scale).astype(bf16)
    dq = jnp.einsum("shqk,skhd->sqhd", dsb, k4, preferred_element_type=f32).reshape(
        total_rows, width
    )
    key_terms = jnp.einsum("shqk,sqhd->skhd", dsb, q4, preferred_element_type=f32).reshape(
        slots, frames, width
    )
    value_terms = jnp.einsum("shqk,sqhd->skhd", pb, dc4, preferred_element_type=f32).reshape(
        slots, frames, width
    )
    dk, dv = (
        lax.psum_scatter(key_terms, "seq", scatter_dimension=1, tiled=True),
        lax.psum_scatter(value_terms, "seq", scatter_dimension=1, tiled=True),
    )
    dk = dk.reshape(total_rows, width)
    dv = dv.reshape(total_rows, width)
    dqb = dq.astype(bf16)
    dkb = dk.astype(bf16)
    dvb = dv.astype(bf16)
    dh1 = (tdot(dqb, wq.T) + tdot(dkb, wk.T) + tdot(dvb, wv.T)).reshape(slots, count, width)
    grad_x = dmid + norm_back(dh1, n1, r1, g1.astype(f32))
    first_cols = h1b.T
    ctx_cols = ctxb.T
    second_cols = h2b.T
    stacked = lax.psum_scatter(
        jnp.concatenate(
            [
                tdot(first_cols, dqb),
                tdot(first_cols, dkb),
                tdot(first_cols, dvb),
                tdot(ctx_cols, dmidb),
                tdot(second_cols, dpreb),
            ],
            axis=1,
        ),
        ("clip", "seq"),
        scatter_dimension=0,
        tiled=True,
    )
    act_cols = actb.T
    grad_fc2 = lax.psum_scatter(
        tdot(act_cols, gyb), ("clip", "seq"), scatter_dimension=0, tiled=True
    )
    grad_q = stacked[:, 0:width]
    grad_k = stacked[:, width : 2 * width]
    grad_v = stacked[:, 2 * width : 3 * width]
    grad_o = stacked[:, 3 * width : 4 * width]
    grad_fc1 = stacked[:, 4 * width :]
    n1f = n1.reshape(total_rows, width)
    n2f = n2.reshape(total_rows, width)
    dh1f = dh1.reshape(total_rows, width)
    dh2f = dh2.reshape(total_rows, width)
    dmidf = dmid.reshape(total_rows, width)
    gyf = gy.reshape(total_rows, width)
    vectors = (
        lax.psum_scatter(
            jnp.sum(dh1f * n1f, axis=0), ("clip", "seq"), scatter_dimension=0, tiled=True
        ),
        lax.psum_scatter(jnp.sum(dh1f, axis=0), ("clip", "seq"), scatter_dimension=0, tiled=True),
        lax.psum_scatter(jnp.sum(dq, axis=0), ("clip", "seq"), scatter_dimension=0, tiled=True),
        lax.psum_scatter(jnp.sum(dv, axis=0), ("clip", "seq"), scatter_dimension=0, tiled=True),
        lax.psum_scatter(jnp.sum(dmidf, axis=0), ("clip", "seq"), scatter_dimension=0, tiled=True),
        lax.psum_scatter(
            jnp.sum(dh2f * n2f, axis=0), ("clip", "seq"), scatter_dimension=0, tiled=True
        ),
        lax.psum_scatter(jnp.sum(dh2f, axis=0), ("clip", "seq"), scatter_dimension=0, tiled=True),
        lax.psum_scatter(jnp.sum(dpre, axis=0), ("clip", "seq"), scatter_dimension=0, tiled=True),
        lax.psum_scatter(jnp.sum(gyf, axis=0), ("clip", "seq"), scatter_dimension=0, tiled=True),
    )
    return (
        result,
        grad_x,
        vectors[0],
        vectors[1],
        grad_q,
        vectors[2],
        grad_k,
        grad_v,
        vectors[3],
        grad_o,
        vectors[4],
        vectors[5],
        vectors[6],
        grad_fc1,
        vectors[7],
        grad_fc2,
        vectors[8],
    )


def solution(mesh):
    in_specs = (
        P("clip", "seq", None),
        P("clip"),
        P(("clip", "seq")),
        P(("clip", "seq")),
        P(("clip", "seq"), None),
        P(("clip", "seq")),
        P(("clip", "seq"), None),
        P(("clip", "seq"), None),
        P(("clip", "seq")),
        P(("clip", "seq"), None),
        P(("clip", "seq")),
        P(("clip", "seq")),
        P(("clip", "seq")),
        P(("clip", "seq"), None),
        P(("clip", "seq")),
        P(("clip", "seq"), None),
        P(("clip", "seq")),
        P("clip", "seq", None),
    )
    out_specs = (
        P("clip", "seq", None),
        P("clip", "seq", None),
        P(("clip", "seq")),
        P(("clip", "seq")),
        P(("clip", "seq"), None),
        P(("clip", "seq")),
        P(("clip", "seq"), None),
        P(("clip", "seq"), None),
        P(("clip", "seq")),
        P(("clip", "seq"), None),
        P(("clip", "seq")),
        P(("clip", "seq")),
        P(("clip", "seq")),
        P(("clip", "seq"), None),
        P(("clip", "seq")),
        P(("clip", "seq"), None),
        P(("clip", "seq")),
    )
    return jax.shard_map(
        on_device, mesh=mesh, in_specs=in_specs, out_specs=out_specs, check_vma=False
    )
```

profile of v0, /device:TPU:0, one launch (start us, length us, event | category | flops | bytes accessed | tf_op | source)
XLA Modules:
  0.0 800.6 jit_solution(1826645265059283352)
XLA Ops:
  14.4 0.8 dynamic-update-slice.3
  15.2 0.8 dynamic-update-slice.2
  18.5 0.8 dynamic-update-slice.7
  19.4 42.5 %all-reduce.19 = (bf16[768]{0:T(1024)(128)(2,1)S(1)}, bf16[768]{0:T(1024)(128)(2,1)S(1)}, bf16[768]{0:T(1024)(128)(2,1)S(1)}, bf16[768]{0:T(1024)(128)(2,1)S(1)}...) all-reduce(bf16[768]{0:T(1024)(128)(2,1)S(1)} %dynamic-update-slice, ...), channel_id=1, replica_groups=mesh['clip'=16,'seq'=2] {'clip','seq'}, use_global_device_ids=true, to_apply=%add.1 | all-reduce | flops 9216 | bytes 36864
  63.2 1.0 convert_reduce_fusion
  64.2 1.1 fusion.31
  65.4 1.0 fusion.38
  66.4 1.9 fusion.29
  68.3 1.6 fusion.21
  69.9 7.3 all_gather.55
  77.5 46.5 %all-gather.11.cloned.1.call-done = bf16[768,768]{1,0:T(8,128)(2,1)} async-done(((bf16[24,768]{1,0:T(8,128)(2,1)}), bf16[768,768]{1,0:T(8,128)(2,1)}) %all-gather.11.cloned.1.call-update) | async-done | bytes 1179664 | tf_op jit(solution)/shard_map/all_gather | solution.py:71
  124.0 1.6 convolution_convert_fusion.2
  125.6 7.9 all_gather.59
  133.7 46.2 %all-gather.9.cloned.1.call-done = bf16[768,768]{1,0:T(8,128)(2,1)} async-done(((bf16[24,768]{1,0:T(8,128)(2,1)}), bf16[768,768]{1,0:T(8,128)(2,1)}) %all-gather.9.cloned.1.call-update) | async-done | bytes 1179664 | tf_op jit(solution)/shard_map/all_gather | solution.py:69
  179.9 1.6 fusion.22
  183.8 51.9 %all-gather.13.cloned.1.call-done = bf16[768,768]{1,0:T(8,128)(2,1)} async-done(((bf16[24,768]{1,0:T(8,128)(2,1)}), bf16[768,768]{1,0:T(8,128)(2,1)}) %all-gather.13.cloned.1.call-update) | async-done | bytes 1179664 | tf_op jit(solution)/shard_map/all_gather | solution.py:74
  235.7 1.7 fusion.59
  237.8 63.2 %all-gather.15.cloned.1.call-done = bf16[768,3072]{1,0:T(8,128)(2,1)} async-done(((bf16[24,3072]{1,0:T(8,128)(2,1)}), bf16[768,3072]{1,0:T(8,128)(2,1)}) %all-gather.15.cloned.1.call-update) | async-done | bytes 4718608 | tf_op jit(solution)/shard_map/all_gather | solution.py:78
  301.0 7.5 fusion.3
  308.5 57.2 %all-gather.17.cloned.1.call-done = bf16[3072,768]{1,0:T(8,128)(2,1)} async-done(((bf16[96,768]{1,0:T(8,128)(2,1)}), bf16[3072,768]{1,0:T(8,128)(2,1)}) %all-gather.17.cloned.1.call-update) | async-done | bytes 4718608 | tf_op jit(solution)/shard_map/all_gather | solution.py:80
  365.7 5.3 fusion.62
  371.0 2.3 fusion.52
  373.8 1.3 div.33
  376.0 3.2 fusion.63
  379.3 1.5 fusion.54
  382.2 1.1 reshape.206
  383.3 1.4 copy.75
  384.7 1.2 fusion.64
  385.9 10.7 %fusion.23 = f32[2,12,64,128]{3,2,1,0:T(8,128)} fusion(bf16[2,64,12,64]{1,3,2,0:T(8,128)(2,1)S(1)} %copy-done.13, f32[2,12,64,128]{3,2,1,0:T(8,128)} %fusion.64, f32[2,12,64,128]{3,2,1,0:T(8,128)S(1)} %get-tuple-element.58, f32[2,12,64]{2,1,0:T(8,128)S(1)} %log_add_fusion), kind=kOutput, calls=%fused_computation.50 | convolution fusion | flops 26543744 | bytes 2562048 | tf_op jit(solution)/shard_map/shqk,sqhd->skhd/dot_general | solution.py:134
  396.6 2.3 copy.74
  399.4 1.2 copy.76
  401.6 10.3 %fusion.55 = (f32[12,64]{1,0:T(8,128)}, bf16[2,64,12,64]{3,1,2,0:T(8,128)(2,1)S(1)}) fusion(bf16[2,128,12,64]{1,3,2,0:T(8,128)(2,1)S(1)} %bitcast.108, f32[2,12,64,128]{3,2,1,0:T(8,128)} %fusion.64, f32[2,12,64,128]{3,2,1,0:T(8,128)S(1)} %get-tuple-element.58, f32[2,12,64]{2,1,0:T(8,128)S(1)} %log_add_fusion), kind=kOutput, calls=%fused_computation.104 | convolution fusion | flops 26739584 | bytes 2171904 | tf_op jit(solution)/shard_map/shqk,skhd->sqhd/dot_general | solution.py:131
  412.5 2.0 convolution_dynamic-update-slice_fusion.2
  414.9 1.0 convert_element_type.142
  416.0 2.0 bitcast_dynamic-update-slice_fusion.1
  418.0 16.8 %reduce-scatter.7.cloned.1.call-done = f32[2,64,768]{2,1,0:T(8,128)} async-done(((f32[2,128,768]{2,1,0:T(8,128)}), f32[2,64,768]{2,1,0:T(8,128)}) %reduce-scatter.7.cloned.1.call-update) | async-done | bytes 393232 | tf_op jit(solution)/shard_map/reduce_scatter | solution.py:142
  434.7 1.2 fusion.57
  435.9 1.9 bitcast_dynamic-update-slice_fusion
  437.8 1.9 convolution_dynamic-update-slice_fusion.1
  439.8 5.2 convolution_dynamic-update-slice_fusion
  445.0 0.9 copy-done.19
  445.9 5.1 fusion.66
  454.6 40.4 %all-reduce.18 = (f32[768]{0:T(1024)S(1)}, f32[768]{0:T(1024)S(1)}, f32[768]{0:T(1024)S(1)}, f32[768]{0:T(1024)S(1)}, f32[768]{0:T(1024)S(1)}, /*index=5*/f32[76...) all-reduce(f32[768]{0:T(1024)S(1)} %get-tuple-element.21, ...), channel_id=4, replica_groups=mesh['clip'=16,'seq'=2] {'clip','seq'}, use_global_device_ids=true, to_apply=%region_14.0.clone | all-reduce | flops 9216 | bytes 73728
  500.6 0.9 multiply_add_fusion
  501.5 150.5 %reduce-scatter.9.cloned.1.call-done = f32[24,6144]{1,0:T(8,128)} async-done(((f32[768,6144]{1,0:T(8,128)}), f32[24,6144]{1,0:T(8,128)}) %reduce-scatter.9.cloned.1.call-update) | async-done | bytes 589840 | tf_op jit(solution)/shard_map/reduce_scatter | solution.py:154
  652.0 1.7 slice.24
  653.7 1.7 fusion.56
  655.4 138.4 %reduce-scatter.11.cloned.1.call-done = f32[96,768]{1,0:T(8,128)} async-done(((f32[3072,768]{1,0:T(8,128)}), f32[96,768]{1,0:T(8,128)}) %reduce-scatter.11.cloned.1.call-update) | async-done | bytes 294928 | tf_op jit(solution)/shard_map/reduce_scatter | solution.py:170
  (173 shorter events, 28.0 us)
Async XLA Ops:
  7.2 61.1 %all-gather.7.cloned.1.call-start = ((), (), s32[]{:S(2)}) async-start(), calls=%async_computation.4 | async-start | bytes 1216512 | tf_op jit(solution)/shard_map/all_gather | solution.py:72
  7.9 116.1 %all-gather.11.cloned.1.call-start = ((), (), s32[]{:S(2)}) async-start(), calls=%async_computation.6 | async-start | bytes 1216512 | tf_op jit(solution)/shard_map/all_gather | solution.py:71
  8.7 171.2 %all-gather.9.cloned.1.call-start = ((), (), s32[]{:S(2)}) async-start(), calls=%async_computation.5 | async-start | bytes 1216512 | tf_op jit(solution)/shard_map/all_gather | solution.py:69
  9.4 226.3 %all-gather.13.cloned.1.call-start = ((), (), s32[]{:S(2)}) async-start(), calls=%async_computation.7 | async-start | bytes 1216512 | tf_op jit(solution)/shard_map/all_gather | solution.py:74
  10.0 291.0 %all-gather.15.cloned.1.call-start = ((), (), s32[]{:S(2)}) async-start(), calls=%async_computation.8 | async-start | bytes 4866048 | tf_op jit(solution)/shard_map/all_gather | solution.py:78
  10.6 355.1 %all-gather.17.cloned.1.call-start = ((), (), s32[]{:S(2)}) async-start(), calls=%async_computation.9 | async-start | bytes 4866048 | tf_op jit(solution)/shard_map/all_gather | solution.py:80
  11.1 403.8 %reduce-scatter.5.cloned.1.call-start = ((), (), s32[]{:S(2)}) async-start(), calls=%async_computation.10 | async-start | bytes 1179648 | tf_op jit(solution)/shard_map/reduce_scatter | solution.py:141
  11.9 56.5 %copy-start.40 = (f32[2]{0:T(128)}, f32[2]{0:T(128)S(1)}, u32[]{:S(2)}) copy-start(f32[2]{0:T(128)S(1)} %convert_element_type.112) | copy-start | bytes 28
  61.9 6.5 copy-start.22
  61.9 175.7 %copy-start.24 = (f32[768]{0:T(1024)}, f32[768]{0:T(1024)S(1)}, u32[]{:S(2)}) copy-start(f32[768]{0:T(1024)S(1)} %convert_element_type.127) | copy-start | bytes 9220
  64.2 4.1 copy-start.27
  65.4 11.9 %copy-start.32 = (f32[2,64]{1,0:T(2,128)}, f32[2,64]{1,0:T(2,128)S(1)}, u32[]{:S(2)}) copy-start(f32[2,64]{1,0:T(2,128)S(1)} %add_rsqrt_fusion.1) | copy-start | bytes 1540
  66.4 299.3 %copy-start.18 = (bf16[2,64,768]{2,1,0:T(8,128)(2,1)}, bf16[2,64,768]{2,1,0:T(8,128)(2,1)S(1)}, u32[]{:S(2)}) copy-start(bf16[2,64,768]{2,1,0:T(8,128)(2,1)S(1)} %fusion.38) | copy-start | bytes 589828
  133.7 48.6 %copy-start.14 = (bf16[2,128,768]{1,2,0:T(8,128)(2,1)}, bf16[2,128,768]{1,2,0:T(8,128)(2,1)S(1)}, u32[]{:S(2)}) copy-start(bf16[2,128,768]{1,2,0:T(8,128)(2,1)S(1)} %copy.67) | copy-start | bytes 1179652
  182.3 1.5 copy-start.12
  182.8 52.9 %copy-start = (bf16[2,64,768]{2,1,0:T(8,128)(2,1)S(1)}, bf16[2,64,768]{2,1,0:T(8,128)(2,1)}, u32[]{:S(2)}) copy-start(bf16[2,64,768]{2,1,0:T(8,128)(2,1)} %param.18) | copy-start | bytes 589828
  183.8 53.8 %copy-start.8 = (bf16[2,12,64,64]{3,2,1,0:T(8,128)(2,1)}, bf16[2,12,64,64]{3,2,1,0:T(8,128)(2,1)S(1)}, u32[]{:S(2)}) copy-start(bf16[2,12,64,64]{3,2,1,0:T(8,128)(2,1)S(1)} %convolution_convert_fusion) | copy-start | bytes 589828
  237.6 63.3 %copy-start.37 = (f32[2,64]{1,0:T(2,128)}, f32[2,64]{1,0:T(2,128)S(1)}, u32[]{:S(2)}) copy-start(f32[2,64]{1,0:T(2,128)S(1)} %add_rsqrt_fusion) | copy-start | bytes 1540
  237.8 70.7 %copy-start.20 = (bf16[2,64,768]{2,1,0:T(8,128)(2,1)}, bf16[2,64,768]{2,1,0:T(8,128)(2,1)S(1)}, u32[]{:S(2)}) copy-start(bf16[2,64,768]{2,1,0:T(8,128)(2,1)S(1)} %get-tuple-element.43) | copy-start | bytes 589828
  365.7 5.3 copy-start.1
  365.7 5.3 copy-start.25
  371.0 2.3 copy-start.10
  376.0 3.3 copy-start.17
  376.0 3.3 copy-start.26
  376.0 3.3 copy-start.29
  376.0 3.3 copy-start.38
  376.0 3.3 copy-start.41
  376.0 3.3 copy-start.42
  379.3 2.3 copy-start.5
  382.2 3.7 copy-start.13
  398.9 35.8 %reduce-scatter.7.cloned.1.call-start = ((), (), s32[]{:S(2)}) async-start(), calls=%async_computation.11 | async-start | bytes 1179648 | tf_op jit(solution)/shard_map/reduce_scatter | solution.py:142
  399.4 1.2 copy-start.9
  400.6 251.4 %reduce-scatter.9.cloned.1.call-start = ((), (), s32[]{:S(2)}) async-start(), calls=%async_computation.12 | async-start | bytes 19464192 | tf_op jit(solution)/shard_map/reduce_scatter | solution.py:154
  437.8 1.9 copy-start.11
  437.8 1.9 copy-start.21
  445.0 348.8 %reduce-scatter.11.cloned.1.call-start = ((), (), s32[]{:S(2)}) async-start(), calls=%async_computation.13 | async-start | bytes 9732096 | tf_op jit(solution)/shard_map/reduce_scatter | solution.py:170
  451.0 1.3 copy-start.4
  451.1 1.8 copy-start.3
  452.3 1.5 copy-start.2
  452.3 1.6 copy-start.16
  452.3 1.6 copy-start.23
  453.4 1.2 copy-start.30
  453.4 1.2 copy-start.31
  453.4 1.2 copy-start.34
  453.5 1.2 copy-start.35
  453.5 46.9 %copy-start.28 = (f32[2,64]{1,0:T(2,128)S(1)}, f32[2,64]{1,0:T(2,128)}, u32[]{:S(2)}) copy-start(f32[2,64]{1,0:T(2,128)} %copy-done.27) | copy-start | bytes 1540
  453.5 46.9 %copy-start.33 = (f32[2,64]{1,0:T(2,128)S(1)}, f32[2,64]{1,0:T(2,128)}, u32[]{:S(2)}) copy-start(f32[2,64]{1,0:T(2,128)} %copy-done.32) | copy-start | bytes 1540
  453.9 46.7 %copy-start.7 = (f32[2,64,768]{2,1,0:T(8,128)S(1)}, f32[2,64,768]{2,1,0:T(8,128)}, u32[]{:S(2)}) copy-start(f32[2,64,768]{2,1,0:T(8,128)} %copy-done.6) | copy-start | bytes 1179652
  (5 other events, 4.5 us)
Sparse Core Ops, SparseCore 0:
  10.9 57.0 all-gather.6
  70.9 53.0 all-gather.10
  126.9 52.9 all-gather.8
  182.7 52.9 all-gather.12
  238.4 62.4 all-gather.14
  303.7 61.9 all-gather.16
  399.1 15.8 reduce-scatter.4
  417.2 17.5 reduce-scatter.6
  445.1 206.8 reduce-scatter.8
  658.3 135.3 reduce-scatter.10
where the time goes:
time: 802 us; the launch traced here: 801 us
  waiting for transfers between devices  575 us (72%)
  blocking collectives  98.1 us (12%)
  matrix products  68.8 us (9%)
  local copies, waits for them, and re-layouts  29.6 us (4%)
  between operations  14.8 us (2%)
  other arithmetic  14.1 us (2%)
    reduce_scatter x1, waiting for transfers between devices, on_device(): lax.psum_scatter(jnp.concatenate([tdot(first_cols, dqb), tdot(first_cols,...  150 us
    reduce_scatter x1, waiting for transfers between devices, on_device(): lax.psum_scatter(tdot(act_cols, gyb), ('clip', 'seq'), scatter_dimension=...  138 us
    unnamed x2, blocking collectives  82.9 us
    all_gather x1, waiting for transfers between devices, on_device(): lax.all_gather(w_fc1, ('clip', 'seq'), axis=0, tiled=True)  63.2 us
    all_gather x1, waiting for transfers between devices, on_device(): lax.all_gather(w_fc2, ('clip', 'seq'), axis=0, tiled=True)  57.2 us
    all_gather x1, waiting for transfers between devices, on_device(): lax.all_gather(w_o, ('clip', 'seq'), axis=0, tiled=True)  51.9 us
    all_gather x1, waiting for transfers between devices, on_device(): lax.all_gather(w_k, ('clip', 'seq'), axis=0, tiled=True)  46.5 us
    all_gather x1, waiting for transfers between devices, on_device(): lax.all_gather(w_q, ('clip', 'seq'), axis=0, tiled=True)  46.2 us
  transfers between devices with their start and end apart: 10, of which 9 were waited for; matrix products, arithmetic and copies ran while one was open for 8% of the time, Pallas kernels for 0%

commit v1 on v0

--- a/solution.py
+++ b/solution.py
@@ -1,8 +1,12 @@
+import functools
 import math
 
 import jax
 import jax.numpy as jnp
 from jax import lax
+from jax.experimental import pallas as pl
+from jax.experimental.pallas import tpu as pltpu
+from jax.sharding import Mesh
 from jax.sharding import PartitionSpec as P
 
 HEADS = 12
@@ -40,7 +44,7 @@
     return jnp.dot(left, right, preferred_element_type=jnp.float32)
 
 
-def on_device(
+def on_device_gathered(
     inputs,
     micro_live,
     ln1_gain,
@@ -217,46 +221,492 @@
     )
 
 
+F32 = jnp.float32
+BF16 = jnp.bfloat16
+SCALE = 1.0 / math.sqrt(HD)
+SWAP = ((0, 1), (1, 0))
+VMEM_LIMIT = 56 * 1024 * 1024
+
+
+def nt_dot(left, right):
+    return lax.dot_general(left, right, (((1,), (1,)), ((), ())), preferred_element_type=F32)
+
+
+def tn_dot(left, right):
+    return lax.dot_general(left, right, (((0,), (0,)), ((), ())), preferred_element_type=F32)
+
+
+def head_masks(rows, width, dtype):
+    lanes = lax.broadcasted_iota(jnp.int32, (rows, width), 1)
+    return [
+        jnp.where((lanes >= h * HD) & (lanes < (h + 1) * HD), 1.0, 0.0).astype(F32).astype(dtype)
+        for h in range(width // HD)
+    ]
+
+
+def attention_forward(slots, x, gain, shift, weight, bias):
+    part = weight.shape[1] // 3
+    frames = x.shape[0] // slots
+    h1, _, _ = layer_norm(x.astype(F32), gain, shift)
+    h1b = h1.astype(BF16)
+    qkv = (tdot(h1b, weight) + bias).astype(BF16)
+    q, k, v = qkv[:, :part], qkv[:, part : 2 * part], qkv[:, 2 * part :]
+    masks = head_masks(frames, part, BF16)
+    masks32 = head_masks(frames, part, F32)
+    ctx_rows, all_probs = [], []
+    for s in range(slots):
+        rows = slice(s * frames, (s + 1) * frames)
+        qs, ks, vs = q[rows], k[rows], v[rows]
+        ctx = None
+        for mask, mask32 in zip(masks, masks32):
+            scores = nt_dot(qs * mask, ks) * SCALE
+            peak = jnp.max(scores, axis=-1, keepdims=True)
+            lse = peak + jnp.log(jnp.sum(jnp.exp(scores - peak), axis=-1, keepdims=True))
+            probs = jnp.exp(scores - lse)
+            all_probs.append(probs)
+            term = tdot(probs.astype(BF16), vs) * mask32
+            ctx = term if ctx is None else ctx + term
+        ctx_rows.append(ctx)
+    ctxb = jnp.concatenate(ctx_rows, axis=0).astype(BF16)
+    return h1b, q, k, v, jnp.stack(all_probs), ctxb
+
+
+def attention_backward(slots, dctx, q, k, v, probs, weight):
+    part = q.shape[1]
+    frames = q.shape[0] // slots
+    masks = head_masks(frames, part, BF16)
+    masks32 = head_masks(frames, part, F32)
+    dqs, dks, dvs = [], [], []
+    for s in range(slots):
+        rows = slice(s * frames, (s + 1) * frames)
+        ds_, qs, ks, vs = dctx[rows], q[rows], k[rows], v[rows]
+        dq = dk = dv = None
+        for h, (mask, mask32) in enumerate(zip(masks, masks32)):
+            p = probs[s * len(masks) + h]
+            dprob = nt_dot(ds_ * mask, vs)
+            delta = jnp.sum(p * dprob, axis=-1, keepdims=True)
+            dsb = (p * (dprob - delta) * SCALE).astype(BF16)
+            tq = tdot(dsb, ks) * mask32
+            tk = tn_dot(dsb, qs) * mask32
+            tv = tn_dot(p.astype(BF16), ds_) * mask32
+            dq = tq if dq is None else dq + tq
+            dk = tk if dk is None else dk + tk
+            dv = tv if dv is None else dv + tv
+        dqs.append(dq)
+        dks.append(dk)
+        dvs.append(dv)
+    dq = jnp.concatenate(dqs, axis=0)
+    dk = jnp.concatenate(dks, axis=0)
+    dv = jnp.concatenate(dvs, axis=0)
+    grads = jnp.concatenate([dq, dk, dv], axis=1).astype(BF16)
+    dh1 = nt_dot(grads, weight).astype(BF16)
+    return (
+        grads,
+        dh1,
+        jnp.sum(dq, axis=0, keepdims=True)[None],
+        jnp.sum(dv, axis=0, keepdims=True)[None],
+    )
+
+
+def out_projection(x, ctx, weight, bias, gain, shift):
+    mid = x.astype(F32) + tdot(ctx, weight) + bias
+    h2, _, _ = layer_norm(mid, gain, shift)
+    return mid, h2.astype(BF16)
+
+
+def feed_forward(h2b, gyb, first, bias, second):
+    pre = tdot(h2b, first) + bias
+    phi = 0.5 * (1.0 + lax.erf(pre * 0.7071067811865476))
+    act = (pre * phi).astype(BF16)
+    slope = phi + pre * jnp.exp(-0.5 * pre * pre) * 0.3989422804014327
+    dpre = nt_dot(gyb, second) * slope
+    dpreb = dpre.astype(BF16)
+    dh2 = nt_dot(dpreb, first).astype(BF16)
+    return act, dpreb, dh2, jnp.sum(dpre, axis=0, keepdims=True)[None]
+
+
+def middle_backward(dh2, mid, gyb, weight, gain):
+    gy = gyb.astype(F32)
+    _, normed, inv = layer_norm(mid, gain, gain)
+    dmid = gy + norm_back(dh2, normed, inv, gain)
+    dmidb = dmid.astype(BF16)
+    dctx = nt_dot(dmidb, weight).astype(BF16)
+    sums = [
+        jnp.sum(dmid, axis=0, keepdims=True),
+        jnp.sum(dh2 * normed, axis=0, keepdims=True),
+        jnp.sum(dh2, axis=0, keepdims=True),
+        jnp.sum(gy, axis=0, keepdims=True),
+    ]
+    return dmid, dmidb, dctx, *sums
+
+
+def input_backward(dh1, dmid, x, gain):
+    _, normed, inv = layer_norm(x.astype(F32), gain, gain)
+    grad_x = dmid + norm_back(dh1, normed, inv, gain)
+    return (
+        grad_x,
+        jnp.sum(dh1 * normed, axis=0, keepdims=True),
+        jnp.sum(dh1, axis=0, keepdims=True),
+    )
+
+
+def run_kernel(fn, steps, cut_ins, whole_ins, outs, name, flops):
+    def spec(shape, cut):
+        block = (shape[0] // steps,) + tuple(shape[1:]) if cut else tuple(shape)
+        zeros = (0,) * (len(shape) - 1)
+        return pl.BlockSpec(block, (lambda i: (i,) + zeros) if cut else (lambda i: (0,) + zeros))
+
+    count = len(cut_ins) + len(whole_ins)
+
+    def kernel(*refs):
+        values = fn(*[r[...] for r in refs[:count]])
+        for ref, value in zip(refs[count:], values):
+            ref[...] = value
+
+    moved = sum(a.size * a.dtype.itemsize for a in (*cut_ins, *whole_ins))
+    moved += sum(math.prod(s) * jnp.dtype(d).itemsize for s, d in outs)
+    return pl.pallas_call(
+        kernel,
+        grid=(steps,),
+        in_specs=[spec(a.shape, True) for a in cut_ins] + [spec(a.shape, False) for a in whole_ins],
+        out_specs=[spec(s, True) for s, _ in outs],
+        out_shape=[jax.ShapeDtypeStruct(s, d) for s, d in outs],
+        compiler_params=pltpu.CompilerParams(
+            dimension_semantics=("arbitrary",), vmem_limit_bytes=VMEM_LIMIT
+        ),
+        cost_estimate=pl.CostEstimate(flops=flops, bytes_accessed=moved, transcendentals=0),
+        name=name,
+    )(*cut_ins, *whole_ins)
+
+
+def swap(value, axis):
+    return lax.ppermute(value, axis, SWAP)
+
+
+def pick(value, index, axis=0):
+    return lax.dynamic_index_in_dim(value, index, axis, keepdims=False)
+
+
+def ordered(own, other, index, axis):
+    return jnp.where(
+        index == 0, jnp.stack([own, other], axis), jnp.stack([other, own], axis)
+    )
+
+
+def gather_pair(value, axis_name, index, axis):
+    return ordered(value, swap(value, axis_name), index, axis)
+
+
+def trade_pair(value, axis_name, index, axis):
+    other = swap(pick(value, 1 - index, axis), axis_name)
+    return ordered(pick(value, index, axis), other, index, axis)
+
+
+def ring_gather(block, ring, place, rest_sizes):
+    z, x = place
+    step = tuple((i, (i + 1) % ring) for i in range(ring))
+    starts = [sum(rest_sizes[:n]) for n in range(len(rest_sizes))]
+    outs = [jnp.zeros((ring, 2, n, block.shape[1]), block.dtype) for n in rest_sizes]
+    for s in range(ring):
+        if s:
+            block = lax.ppermute(block, "z", step)
+        pair = gather_pair(block, "x", x, 0)
+        at = lax.rem(z - s + ring, ring)
+        for n, (start, size) in enumerate(zip(starts, rest_sizes)):
+            outs[n] = lax.dynamic_update_slice(
+                outs[n], pair[None, :, start : start + size], (at, 0, 0, 0)
+            )
+    return outs
+
+
+def ring_scatter(grad, ring, place):
+    z, x = place
+    step = tuple((i, (i + 1) % ring) for i in range(ring))
+    cut = grad.reshape(ring, 2, -1, grad.shape[-1])
+    own = pick(cut, x, 1)
+    other = swap(pick(cut, 1 - x, 1), "x")
+    total = None
+    for s in range(1, ring + 1):
+        at = lax.rem(z - s + ring, ring)
+        term = pick(own, at).astype(F32) + pick(other, at).astype(F32)
+        total = term if total is None else total + term
+        if s < ring:
+            total = lax.ppermute(total.astype(BF16), "z", step).astype(F32)
+    return total
+
+
+def on_device_split(
+    ring,
+    inputs,
+    micro_live,
+    ln1_gain,
+    ln1_shift,
+    w_q,
+    b_q,
+    w_k,
+    w_v,
+    b_v,
+    w_o,
+    b_o,
+    ln2_gain,
+    ln2_shift,
+    w_fc1,
+    b_fc1,
+    w_fc2,
+    b_fc2,
+    grad_out,
+):
+    z, x, c, y = (lax.axis_index(a) for a in ("z", "x", "c", "y"))
+    place = (z, x)
+    me = 2 * c + y
+    slots, count, width = inputs.shape
+    rows = slots * count
+    shard = w_q.shape[0]
+    units = w_fc2.shape[0]
+    groups = 2 * ring
+    part = width // 4
+    wide = w_fc1.shape[1] // 4
+    all_slots, frames = 2 * slots, 2 * count
+    all_rows = all_slots * frames
+
+    def gather_rows(value):
+        both = gather_pair(value, "y", y, 1).reshape(slots, frames, width)
+        return gather_pair(both, "c", c, 0).reshape(all_rows, width)
+
+    def scatter_rows(value):
+        cut = value.reshape(2, slots, 2, count, width)
+        own = pick(cut, c).astype(F32)
+        half = own + swap(pick(cut, 1 - c), "c").astype(F32)
+        other = swap(pick(half, 1 - y, 1).astype(BF16), "y").astype(F32)
+        return (pick(half, y, 1) + other).reshape(rows, width)
+
+    def trade_four(value):
+        cut = value.reshape(2, 2, *value.shape[1:])
+        return trade_pair(trade_pair(cut, "y", y, 1), "c", c, 0).reshape(value.shape)
+
+    columns = jnp.stack([w_q, w_k, w_v], 1).reshape(shard, 3, 4, part)
+    columns = columns.transpose(2, 0, 1, 3).reshape(4, shard, 3 * part)
+    vector_rows = jnp.stack([ln1_gain, ln1_shift, b_q, b_v, b_o, ln2_gain, ln2_shift, b_fc2])
+    vector_rows = jnp.pad(vector_rows, ((0, 8), (0, 3 * part - shard)))
+    vector_rows = jnp.broadcast_to(vector_rows, (4, 16, 3 * part))
+    first = trade_four(jnp.concatenate([columns, vector_rows], axis=1))
+    vectors = first[:, shard : shard + 8, :shard].transpose(1, 0, 2).reshape(8, 4 * shard)
+    vectors = jnp.pad(vectors, ((0, 0), (0, 3 * part - 4 * shard)))
+    units_row = jnp.pad(b_fc1.reshape(1, units), ((0, 7), (0, 3 * part - units)))
+    block = jnp.concatenate([first[:, :shard].reshape(4 * shard, 3 * part), vectors, units_row])
+    x_all = gather_rows(inputs)
+    w_qkv, vectors = ring_gather(block, ring, place, (4 * shard, 16))
+    w_qkv = w_qkv.reshape(width, 3 * part)
+    vectors = vectors.reshape(groups, 16, 3 * part)
+    named = vectors[:, :8, : 4 * shard].transpose(1, 0, 2).reshape(8, 1, width).astype(F32)
+    g1, c1, bq, bv, bo, g2, c2, bf2 = [named[n] for n in range(8)]
+    bf1 = vectors[:, 8, :units].reshape(1, wide).astype(F32)
+
+    columns = w_fc1.reshape(shard, groups, 4, units).transpose(2, 0, 1, 3).reshape(4, shard, wide)
+    block = trade_four(columns).reshape(4 * shard, wide)
+    wo_block, wf1 = ring_gather(
+        jnp.concatenate([w_o, block]), ring, place, (shard, 4 * shard)
+    )
+    wf1 = wf1.reshape(width, wide)
+    wo = gather_pair(wo_block.reshape(groups, shard, width), "y", y, 1)
+    wo = gather_pair(wo, "c", c, 1).reshape(width, width)
+    live = micro_live.astype(F32)[:, None, None]
+    gy_own = (live * grad_out.astype(F32)).astype(BF16)
+    gy_all = gather_rows(gy_own)
+    gy_own = gy_own.reshape(rows, width)
+    (wf2,) = ring_gather(w_fc2, ring, place, (units,))
+    wf2 = wf2.reshape(wide, width)
+
+    bias = jnp.concatenate(
+        [
+            lax.dynamic_slice(bq, (0, me * part), (1, part)),
+            jnp.zeros((1, part), F32),
+            lax.dynamic_slice(bv, (0, me * part), (1, part)),
+        ],
+        axis=1,
+    )
+    steps = 2
+    heads = part // HD
+    h1b, q, k, v, probs, ctxb = run_kernel(
+        functools.partial(attention_forward, all_slots // steps),
+        steps,
+        (x_all,),
+        (g1, c1, w_qkv, bias),
+        [
+            ((all_rows, width), BF16),
+            ((all_rows, part), BF16),
+            ((all_rows, part), BF16),
+            ((all_rows, part), BF16),
+            ((all_slots * heads, frames, frames), F32),
+            ((all_rows, part), BF16),
+        ],
+        "attention_forward",
+        2 * all_rows * part * (3 * width + 2 * frames),
+    )
+
+    def to_rows(value):
+        cut = value.reshape(2, slots, 2, count, part)
+        cut = trade_pair(trade_pair(cut, "y", y, 2), "c", c, 0)
+        return cut.transpose(1, 3, 0, 2, 4).reshape(rows, width)
+
+    def to_heads(value):
+        cut = value.reshape(slots, count, 2, 2, part).transpose(2, 0, 3, 1, 4)
+        return trade_pair(trade_pair(cut, "y", y, 2), "c", c, 0).reshape(all_rows, part)
+
+    ctx_own = to_rows(ctxb)
+    x_own = inputs.reshape(rows, width)
+    mid, h2_own = run_kernel(
+        out_projection,
+        1,
+        (x_own, ctx_own),
+        (wo, bo, g2, c2),
+        [((rows, width), F32), ((rows, width), BF16)],
+        "out_projection",
+        2 * rows * width * width,
+    )
+    h2_all = gather_rows(h2_own.reshape(slots, count, width))
+    act, dpreb, dh2_part, dpre_sum = run_kernel(
+        feed_forward,
+        steps,
+        (h2_all, gy_all),
+        (wf1, bf1, wf2),
+        [
+            ((all_rows, wide), BF16),
+            ((all_rows, wide), BF16),
+            ((all_rows, width), BF16),
+            ((steps, 1, wide), F32),
+        ],
+        "feed_forward",
+        6 * all_rows * width * wide,
+    )
+    dh2 = scatter_rows(dh2_part)
+    grad_fc2 = ring_scatter(tdot(act.T, gy_all).astype(BF16), ring, place)
+    grad_fc1 = ring_scatter(tdot(h2_all.T, dpreb).astype(BF16), ring, place)
+    out_part = scatter_rows(tdot(act, wf2).astype(BF16))
+    result = live * (mid + out_part + bf2).reshape(slots, count, width)
+    result = result.astype(BF16)
+
+    dmid, dmidb, dctx_own, bo_sum, g2_sum, c2_sum, bf2_sum = run_kernel(
+        middle_backward,
+        1,
+        (dh2, mid, gy_own),
+        (wo, g2),
+        [((rows, width), F32), ((rows, width), BF16), ((rows, width), BF16)]
+        + [((1, width), F32)] * 4,
+        "middle_backward",
+        2 * rows * width * width,
+    )
+    dctx = to_heads(dctx_own)
+    dqkv, dh1_part, bq_sum, bv_sum = run_kernel(
+        functools.partial(attention_backward, all_slots // steps),
+        steps,
+        (dctx, q, k, v, probs),
+        (w_qkv,),
+        [
+            ((all_rows, 3 * part), BF16),
+            ((all_rows, width), BF16),
+            ((steps, 1, part), F32),
+            ((steps, 1, part), F32),
+        ],
+        "attention_backward",
+        2 * all_rows * part * (3 * width + 4 * frames),
+    )
+    grad_qkv = ring_scatter(tdot(h1b.T, dqkv).astype(BF16), ring, place)
+    dh1 = scatter_rows(dh1_part)
+    grad_x, g1_sum, c1_sum = run_kernel(
+        input_backward,
+        1,
+        (dh1, dmid, x_own),
+        (g1,),
+        [((rows, width), F32), ((1, width), F32), ((1, width), F32)],
+        "input_backward",
+        rows * width,
+    )
+
+    cut = tdot(ctx_own.T, dmidb).astype(BF16).reshape(groups, 2, 2, shard, width)
+    half = pick(cut, c, 1).astype(F32) + swap(pick(cut, 1 - c, 1), "c").astype(F32)
+    quarter = pick(half, y, 1) + swap(pick(half, 1 - y, 1).astype(BF16), "y").astype(F32)
+    grad_o = ring_scatter(quarter.astype(BF16).reshape(groups * shard, width), ring, place)
+
+    back = grad_fc1.astype(BF16).reshape(4, shard, groups, units)
+    grad_fc1 = trade_four(back).transpose(1, 2, 0, 3).reshape(shard, 4 * wide).astype(F32)
+    back = trade_four(grad_qkv.astype(BF16).reshape(4, shard, 3 * part)).astype(F32)
+    grad_q, grad_k, grad_v = [
+        back[:, :, n * part : (n + 1) * part].transpose(1, 0, 2).reshape(shard, width)
+        for n in range(3)
+    ]
+
+    mine = (jnp.arange(4) == me).astype(F32)[:, None]
+    spread = lambda value: mine * jnp.pad(value, ((0, 0), (0, width - value.shape[1])))
+    packed = jnp.concatenate(
+        [
+            g1_sum,
+            c1_sum,
+            bo_sum,
+            g2_sum,
+            c2_sum,
+            bf2_sum,
+            spread(jnp.sum(dpre_sum, axis=0)),
+            spread(jnp.sum(bq_sum, axis=0)),
+            spread(jnp.sum(bv_sum, axis=0)),
+            jnp.zeros((6, width), F32),
+        ]
+    )
+    for axis in ("c", "y", "x"):
+        packed = packed + swap(packed, axis)
+    hop = 1
+    while hop < ring:
+        packed = packed + lax.ppermute(packed, "z", tuple((i, i ^ hop) for i in range(ring)))
+        hop *= 2
+    spot = (2 * z + x) * 4 + me
+    own = lax.dynamic_slice(packed, (0, spot * shard), (6, shard))
+    grad_bf1 = lax.dynamic_slice(packed, (6 + me, (2 * z + x) * units), (1, units))[0]
+    per_part = part // shard
+    head_row, head_at = spot // per_part, lax.rem(spot, per_part) * shard
+    grad_bq = lax.dynamic_slice(packed, (10 + head_row, head_at), (1, shard))[0]
+    grad_bv = lax.dynamic_slice(packed, (14 + head_row, head_at), (1, shard))[0]
+    return (
+        result,
+        grad_x.reshape(slots, count, width),
+        own[0],
+        own[1],
+        grad_q,
+        grad_bq,
+        grad_k,
+        grad_v,
+        grad_bv,
+        grad_o,
+        own[2],
+        own[3],
+        own[4],
+        grad_fc1,
+        grad_bf1,
+        grad_fc2,
+        own[5],
+    )
+
+
 def solution(mesh):
+    clips, seqs = mesh.shape["clip"], mesh.shape["seq"]
+    ring = clips // 4
+    split = seqs == 2 and clips % 4 == 0 and ring & (ring - 1) == 0
+    if split:
+        names, both = ("z", "x", "c"), ("z", "x", "c", "y")
+        grid = Mesh(mesh.devices.reshape(ring, 2, 2, 2), both)
+        body, seq = functools.partial(on_device_split, ring), "y"
+    else:
+        names, both = ("clip",), ("clip", "seq")
+        grid, body, seq = mesh, on_device_gathered, "seq"
+    rows3 = P(names, seq, None)
+    vector, matrix = P(both), P(both, None)
     in_specs = (
-        P("clip", "seq", None),
-        P("clip"),
-        P(("clip", "seq")),
-        P(("clip", "seq")),
-        P(("clip", "seq"), None),
-        P(("clip", "seq")),
-        P(("clip", "seq"), None),
-        P(("clip", "seq"), None),
-        P(("clip", "seq")),
-        P(("clip", "seq"), None),
-        P(("clip", "seq")),
-        P(("clip", "seq")),
-        P(("clip", "seq")),
-        P(("clip", "seq"), None),
-        P(("clip", "seq")),
-        P(("clip", "seq"), None),
-        P(("clip", "seq")),
-        P("clip", "seq", None),
+        rows3, P(names), vector, vector, matrix, vector, matrix, matrix, vector, matrix,
+        vector, vector, vector, matrix, vector, matrix, vector, rows3,
     )
     out_specs = (
-        P("clip", "seq", None),
-        P("clip", "seq", None),
-        P(("clip", "seq")),
-        P(("clip", "seq")),
-        P(("clip", "seq"), None),
-        P(("clip", "seq")),
-        P(("clip", "seq"), None),
-        P(("clip", "seq"), None),
-        P(("clip", "seq")),
-        P(("clip", "seq"), None),
-        P(("clip", "seq")),
-        P(("clip", "seq")),
-        P(("clip", "seq")),
-        P(("clip", "seq"), None),
-        P(("clip", "seq")),
-        P(("clip", "seq"), None),
-        P(("clip", "seq")),
+        rows3, rows3, vector, vector, matrix, vector, matrix, matrix, vector, matrix,
+        vector, vector, vector, matrix, vector, matrix, vector,
     )
     return jax.shard_map(
-        on_device, mesh=mesh, in_specs=in_specs, out_specs=out_specs, check_vma=False
-    )
+        body, mesh=grid, in_specs=in_specs, out_specs=out_specs, check_vma=False
+    )

time: 802 us -> 247 us (0.31)
  waiting for transfers between devices: 575 us -> 89.8 us
  blocking collectives: 98.1 us -> 0 us
  matrix products: 68.8 us -> 6 us
  starting transfers between devices: 0.39 us -> 48.6 us
  other arithmetic: 14.1 us -> 41.6 us
  Pallas kernels: 0 us -> 25.8 us
  between operations: 14.8 us -> 2.36 us
    reduce_scatter x4 -> x0, waiting for transfers between devices: 306 us -> none  [the longest x1 150 us: on_device(): lax.psum_scatter(jnp.concatenate([tdot(first_cols, dqb), tdot(first_cols,...]
    all_gather x6 -> x0, waiting for transfers between devices: 265 us -> none  [the longest x1 63.2 us: on_device(): lax.all_gather(w_fc1, ('clip', 'seq'), axis=0, tiled=True)]
    ppermute x0 -> x70, waiting for transfers between devices: none -> 89.8 us  [the longest x47 45.7 us: swap(): return lax.ppermute(value, axis, SWAP)]
    unnamed x2 -> x0, blocking collectives: 82.9 us -> none
    ppermute x0 -> x70, starting transfers between devices: none -> 48.6 us  [the longest x47 37.4 us: swap(): return lax.ppermute(value, axis, SWAP)]
    dot_general x18 -> x5, matrix products: 45.2 us -> 6 us  [tdot(): return jnp.dot(left, right, preferred_element_type=jnp.float32)]
    pallas_call x0 -> x6, Pallas kernels: none -> 25.8 us  [run_kernel(): pl.pallas_call(kernel, grid=(steps,), in_specs=[spec(a.shape, True) for a...]
    dot_general x6 -> x0, matrix products: 23.5 us -> none  [the longest x1 10.7 us: on_device(): jnp.einsum('shqk,sqhd->skhd', dsb, q4, preferred_element_type=f32)]
  transfers between devices with their start and end apart: 10 -> 70, of which waited for: 9 -> 30; matrix products, arithmetic and copies ran while one was open for 8% -> 28% of each run, Pallas kernels for 0% -> 7%
where the time goes in v1:
time: 247 us; the launch traced here: 245 us
  waiting for transfers between devices  89.8 us (36%)
  starting transfers between devices  48.6 us (20%)
  other arithmetic  41.6 us (17%)
  local copies, waits for them, and re-layouts  30.9 us (13%)
  Pallas kernels  25.8 us (10%)
  matrix products  6 us (2%)
    ppermute x47, waiting for transfers between devices, swap(): return lax.ppermute(value, axis, SWAP)  45.7 us
    ppermute x47, starting transfers between devices, swap(): return lax.ppermute(value, axis, SWAP)  37.4 us
    ppermute x12, waiting for transfers between devices, ring_scatter(): total = lax.ppermute(total.astype(BF16), 'z', step).astype(F32)  32.4 us
    pallas_call x6, Pallas kernels, run_kernel(): pl.pallas_call(kernel, grid=(steps,), in_specs=[spec(a.shape, True) for a...  25.8 us
    select_n x27, other arithmetic, ordered(): jnp.where(index == 0, jnp.stack([own, other], axis), jnp.stack([other, ow...  13.8 us
    ppermute x9, waiting for transfers between devices, ring_gather(): block = lax.ppermute(block, 'z', step)  11.8 us
    convert_element_type x12, other arithmetic, ring_scatter(): total = lax.ppermute(total.astype(BF16), 'z', step).astype(F32)  10.4 us
    ppermute x9, starting transfers between devices, ring_gather(): block = lax.ppermute(block, 'z', step)  6.54 us
  transfers between devices with their start and end apart: 70, of which 30 were waited for; matrix products, arithmetic and copies ran while one was open for 28% of the time, Pallas kernels for 7%

profile of v1, /device:TPU:0, one launch (start us, length us, event | category | flops | bytes accessed | tf_op | source)
XLA Modules:
  0.0 245.2 jit_solution(4230101953585467781)
XLA Ops:
  0.7 3.0 %collective-permute-start.28 = (bf16[96,768]{1,0:T(8,128)(2,1)}, bf16[96,768]{1,0:T(8,128)(2,1)S(1)}, u32[]{:S(2)}, u32[]{:S(2)}) collective-permute-start(bf16[96,768]{1,0:T(8,128)(2,1)} %param.33), channel_id=1, source_target_pairs={{0,4},{4,0},{1,5},{5,1},{2,6},{6,2},{3,7},{7,3},{8,12},{12,8},{9,1... | collective-permute-start | bytes 442376 | tf_op jit(solution)/shard_map/ppermute | solution.py:383
  3.8 1.6 collective-permute-start.29
  5.4 1.5 collective-permute-start
  11.5 1.6 collective-permute-start.13
  14.1 2.0 collective-permute-done.13
  20.5 1.6 collective-permute-start.16
  22.1 1.5 collective-permute-start.30
  23.8 1.6 collective-permute-start.31
  26.2 4.6 %collective-permute-done.30 = bf16[96,768]{1,0:T(8,128)(2,1)} collective-permute-done((bf16[96,768]{1,0:T(8,128)(2,1)}, bf16[96,768]{1,0:T(8,128)(2,1)}, u32[]{:S(2)}, u32[]{:S(2)}) %collective-permute-start.30) | collective-permute-done | bytes 147488 | tf_op jit(solution)/shard_map/ppermute | solution.py:383
  30.7 1.6 collective-permute-start.5
  34.6 3.1 %collective-permute-done.5 = bf16[112,576]{1,0:T(8,128)(2,1)S(1)} collective-permute-done((bf16[112,576]{1,0:T(8,128)(2,1)S(1)}, bf16[112,576]{1,0:T(8,128)(2,1)S(1)}, u32[]{:S(2)}, u32[]{:S(2)}) %collective-permute-start.5) | collective-permute-done | bytes 129056 | tf_op jit(solution)/shard_map/ppermute | solution.py:412
  38.2 1.5 collective-permute-start.6
  41.0 4.2 %collective-permute-done.6 = bf16[112,576]{1,0:T(8,128)(2,1)S(1)} collective-permute-done((bf16[112,576]{1,0:T(8,128)(2,1)S(1)}, bf16[112,576]{1,0:T(8,128)(2,1)S(1)}, u32[]{:S(2)}, u32[]{:S(2)}) %collective-permute-start.6) | collective-permute-done | bytes 129056 | tf_op jit(solution)/shard_map/ppermute | solution.py:383
  46.0 3.4 %collective-permute-done.7 = bf16[112,576]{1,0:T(8,128)(2,1)S(1)} collective-permute-done((bf16[112,576]{1,0:T(8,128)(2,1)S(1)}, bf16[112,576]{1,0:T(8,128)(2,1)S(1)}, u32[]{:S(2)}, u32[]{:S(2)}) %collective-permute-start.7) | collective-permute-done | bytes 129056 | tf_op jit(solution)/shard_map/ppermute | solution.py:412
  49.4 2.8 %collective-permute-done.17 = bf16[120,768]{1,0:T(8,128)(2,1)S(1)} collective-permute-done((bf16[120,768]{1,0:T(8,128)(2,1)S(1)}, bf16[120,768]{1,0:T(8,128)(2,1)S(1)}, u32[]{:S(2)}, u32[]{:S(2)}) %collective-permute-start.17) | collective-permute-done | bytes 184352 | tf_op jit(solution)/shard_map/ppermute | solution.py:383
  53.0 3.9 %collective-permute-done.18 = bf16[120,768]{1,0:T(8,128)(2,1)} collective-permute-done((bf16[120,768]{1,0:T(8,128)(2,1)S(1)}, bf16[120,768]{1,0:T(8,128)(2,1)}, u32[]{:S(2)}, u32[]{:S(2)}) %collective-permute-start.18) | collective-permute-done | bytes 184352 | tf_op jit(solution)/shard_map/ppermute | solution.py:412
  62.5 3.6 %collective-permute-done.10 = bf16[112,576]{1,0:T(8,128)(2,1)S(1)} collective-permute-done((bf16[112,576]{1,0:T(8,128)(2,1)S(1)}, bf16[112,576]{1,0:T(8,128)(2,1)S(1)}, u32[]{:S(2)}, u32[]{:S(2)}) %collective-permute-start.10) | collective-permute-done | bytes 129056 | tf_op jit(solution)/shard_map/ppermute | solution.py:383
  68.7 5.1 %attention_forward.1 = (bf16[512,768]{1,0:T(8,128)(2,1)}, bf16[512,192]{1,0:T(8,128)(2,1)}, bf16[512,192]{1,0:T(8,128)(2,1)}, bf16[512,192]{1,0:T(8,128)(2,1)}, ...) custom-call(bf16[512,768]{1,0:T(8,128)(2,1)} %bitcast.463, f32[1,768]{1,0:T(1,128)} %squeeze.195.refs_1_.refs_3_, ...), custom_call_target="tpu_custom_call" | custom-call | flops 503316480 | bytes 4038912 | tf_op jit(solution)/shard_map/attention_forward/pallas_call | solution.py:368
  77.5 5.0 %collective-permute-done.21 = bf16[120,768]{1,0:T(8,128)(2,1)S(1)} collective-permute-done((bf16[120,768]{1,0:T(8,128)(2,1)}, bf16[120,768]{1,0:T(8,128)(2,1)S(1)}, u32[]{:S(2)}, u32[]{:S(2)}) %collective-permute-start.21) | collective-permute-done | bytes 184352 | tf_op jit(solution)/shard_map/ppermute | solution.py:383
  83.7 1.5 collective-permute-start.22
  85.2 2.3 maximum_select_fusion.3
  87.7 2.8 %collective-permute-done.22 = bf16[8,24,768]{2,1,0:T(8,128)(2,1)S(1)} collective-permute-done((bf16[8,24,768]{2,1,0:T(8,128)(2,1)S(1)}, bf16[8,24,768]{2,1,0:T(8,128)(2,1)S(1)}, u32[]{:S(2)}, u32[]{:S(2)}) %collective-permute-start.22) | collective-permute-done | bytes 294944 | tf_op jit(solution)/shard_map/ppermute | solution.py:383
  96.1 2.5 %maximum_select_fusion = bf16[8,2,2,24,768]{4,3,2,1,0:T(8,128)(2,1)} fusion(bf16[8,1,2,24,768]{4,3,2,1,0:T(8,128)(2,1)} %bitcast.75, bf16[8,1,2,24,768]{4,3,2,1,0:T(8,128)(2,1)S(1)} %copy_select_fusion, pred[]{:T(512)S(6)} %eq.14), kind=kLoop, calls=%fused_computation.5 | loop fusion | flops 1769472 | bytes 2359297 | tf_op jit(solution)/shard_map/jit(_where)/select_n | solution.py:391
  98.5 2.7 %out_projection.1 = (f32[128,768]{1,0:T(8,128)}, bf16[128,768]{1,0:T(8,128)(2,1)}) custom-call(bf16[128,768]{1,0:T(8,128)(2,1)} %bitcast.424, bf16[128,768]{1,0:T(8,128)(2,1)} %reshape.724.refs_1_, bf16[768,768]{1,0:T(8,128)(2,1)} %bitcast.410, f32[1,768]{1,0:T(1,128)} %squeeze.201.refs_3_, f32[1,768]{1,0:T(1,128)} %squeeze.202.refs_4_, ...), custom_call_target="tpu_custom_call" | custom-call | flops 150994944 | bytes 2171904 | tf_op jit(solution)/shard_map/out_projection/pallas_call | solution.py:368
  103.4 5.4 %collective-permute-done.24 = bf16[2,64,768]{2,1,0:T(8,128)(2,1)S(1)} collective-permute-done((bf16[2,64,768]{2,1,0:T(8,128)(2,1)}, bf16[2,64,768]{2,1,0:T(8,128)(2,1)S(1)}, u32[]{:S(2)}, u32[]{:S(2)}) %collective-permute-start.24) | collective-permute-done | bytes 196640 | tf_op jit(solution)/shard_map/ppermute | solution.py:383
  112.6 5.3 %feed_forward.1 = (bf16[512,768]{1,0:T(8,128)(2,1)}, bf16[512,768]{1,0:T(8,128)(2,1)}, bf16[512,768]{1,0:T(8,128)(2,1)}, f32[2,1,768]{2,1,0:T(1,128)}) custom-call(bf16[512,768]{1,0:T(8,128)(2,1)} %bitcast.464, bf16[512,768]{1,0:T(8,128)(2,1)} %bitcast.461, bf16[768,768]{1,0:T(8,128)(2,1)} %bitcast.439, f32[1,768]{1,0:T(1,128)} %reshape.747.refs_3_, ...), custom_call_target="tpu_custom_call" | custom-call | flops 1811939328 | bytes 6300672 | tf_op jit(solution)/shard_map/feed_forward/pallas_call | solution.py:368
  117.9 1.9 convolution_convert_fusion.4
  129.0 1.5 collective-permute-start.38
  131.9 4.9 %collective-permute-done.38 = bf16[2,64,768]{2,1,0:T(8,128)(2,1)S(1)} collective-permute-done((bf16[2,64,768]{2,1,0:T(8,128)(2,1)S(1)}, bf16[2,64,768]{2,1,0:T(8,128)(2,1)S(1)}, u32[]{:S(2)}, u32[]{:S(2)}) %collective-permute-start.38) | collective-permute-done | bytes 196640 | tf_op jit(solution)/shard_map/ppermute | solution.py:383
  137.6 3.0 %middle_backward.1 = (f32[128,768]{1,0:T(8,128)}, bf16[128,768]{1,0:T(8,128)(2,1)}, bf16[128,768]{1,0:T(8,128)(2,1)}, f32[1,768]{1,0:T(1,128)}, f32[1,768]{1,0:T...) custom-call(f32[128,768]{1,0:T(8,128)} %bitcast.427, f32[128,768]{1,0:T(8,128)} %get-tuple-element.44.refs_1_, ...), custom_call_target="tpu_custom_call" | custom-call | flops 150994944 | bytes 2964480 | tf_op jit(solution)/shard_map/middle_backward/pallas_call | solution.py:368
  142.5 1.5 collective-permute-start.39
  147.8 4.6 %collective-permute-done.66 = bf16[4,96,768]{2,1,0:T(8,128)(2,1)} collective-permute-done((bf16[4,96,768]{2,1,0:T(8,128)(2,1)}, bf16[4,96,768]{2,1,0:T(8,128)(2,1)}, u32[]{:S(2)}, u32[]{:S(2)}) %collective-permute-start.66) | collective-permute-done | bytes 589856 | tf_op jit(solution)/shard_map/ppermute | solution.py:383
  154.7 1.7 fusion.22
  156.3 4.3 %collective-permute-done.67 = bf16[96,768]{1,0:T(8,128)(2,1)S(1)} collective-permute-done((bf16[96,768]{1,0:T(8,128)(2,1)S(1)}, bf16[96,768]{1,0:T(8,128)(2,1)S(1)}, u32[]{:S(2)}, u32[]{:S(2)}) %collective-permute-start.67) | collective-permute-done | bytes 147488 | tf_op jit(solution)/shard_map/ppermute | solution.py:434
  160.6 1.6 fusion.15
  163.1 7.4 %attention_backward.1 = (bf16[512,576]{1,0:T(8,128)(2,1)}, bf16[512,768]{1,0:T(8,128)(2,1)}, f32[2,1,192]{2,1,0:T(1,128)}, f32[2,1,192]{2,1,0:T(1,128)}) custom-call(bf16[512,192]{1,0:T(8,128)(2,1)} %bitcast.459, bf16[512,192]{1,0:T(8,128)(2,1)} %get-tuple-element.49.refs_1_, bf16[512,192]{1,0:T(8,128)(2,1)} %get-tuple-element.50.refs_2_, ...), custom_call_target="tpu_custom_call" | custom-call | flops 553648128 | bytes 3836928 | tf_op jit(solution)/shard_map/attention_backward/pallas_call | solution.py:368
  172.5 2.0 convolution_convert_fusion.3
  179.9 2.5 %collective-permute-start.69 = (bf16[96,768]{1,0:T(8,128)(2,1)S(1)}, bf16[96,768]{1,0:T(8,128)(2,1)S(1)}, u32[]{:S(2)}, u32[]{:S(2)}) collective-permute-start(bf16[96,768]{1,0:T(8,128)(2,1)S(1)} %fusion.13), channel_id=1, source_target_pairs={{0,8},{8,16},{16,24},{24,0},{1,9},{9,17},{17,25},{25,1},{2,10},{10... | collective-permute-start | bytes 442376 | tf_op jit(solution)/shard_map/ppermute | solution.py:434
  182.5 4.5 %collective-permute-done.63 = bf16[96,768]{1,0:T(8,128)(2,1)S(1)} collective-permute-done((bf16[96,768]{1,0:T(8,128)(2,1)S(1)}, bf16[96,768]{1,0:T(8,128)(2,1)S(1)}, u32[]{:S(2)}, u32[]{:S(2)}) %collective-permute-start.63) | collective-permute-done | bytes 147488 | tf_op jit(solution)/shard_map/ppermute | solution.py:434
  189.8 1.7 fusion.11
  194.2 1.5 collective-permute-start.42
  198.7 5.9 %collective-permute-done.49 = bf16[96,576]{1,0:T(8,128)(2,1)S(1)} collective-permute-done((bf16[96,576]{1,0:T(8,128)(2,1)S(1)}, bf16[96,576]{1,0:T(8,128)(2,1)S(1)}, u32[]{:S(2)}, u32[]{:S(2)}) %collective-permute-start.49) | collective-permute-done | bytes 110624 | tf_op jit(solution)/shard_map/ppermute | solution.py:434
  206.4 2.3 input_backward.1
  214.3 1.6 collective-permute-start.56
  217.0 2.9 %collective-permute-done.51 = bf16[96,576]{1,0:T(8,128)(2,1)S(1)} collective-permute-done((bf16[96,576]{1,0:T(8,128)(2,1)S(1)}, bf16[96,576]{1,0:T(8,128)(2,1)S(1)}, u32[]{:S(2)}, u32[]{:S(2)}) %collective-permute-start.51) | collective-permute-done | bytes 110624 | tf_op jit(solution)/shard_map/ppermute | solution.py:434
  226.1 4.9 %collective-permute-done.57 = bf16[24,768]{1,0:T(8,128)(2,1)S(1)} collective-permute-done((bf16[24,768]{1,0:T(8,128)(2,1)S(1)}, bf16[24,768]{1,0:T(8,128)(2,1)S(1)}, u32[]{:S(2)}, u32[]{:S(2)}) %collective-permute-start.57) | collective-permute-done | bytes 36896 | tf_op jit(solution)/shard_map/ppermute | solution.py:434
  231.8 5.1 %collective-permute-done.58 = bf16[24,768]{1,0:T(8,128)(2,1)S(1)} collective-permute-done((bf16[24,768]{1,0:T(8,128)(2,1)S(1)}, bf16[24,768]{1,0:T(8,128)(2,1)S(1)}, u32[]{:S(2)}, u32[]{:S(2)}) %collective-permute-start.58) | collective-permute-done | bytes 36896 | tf_op jit(solution)/shard_map/ppermute | solution.py:434
  239.4 3.3 %collective-permute-done.59 = bf16[24,768]{1,0:T(8,128)(2,1)S(1)} collective-permute-done((bf16[24,768]{1,0:T(8,128)(2,1)S(1)}, bf16[24,768]{1,0:T(8,128)(2,1)S(1)}, u32[]{:S(2)}, u32[]{:S(2)}) %collective-permute-start.59) | collective-permute-done | bytes 36896 | tf_op jit(solution)/shard_map/ppermute | solution.py:434
  (375 shorter events, 96.5 us)
Async XLA Ops:
  0.7 19.0 %collective-permute-start.28 = (bf16[96,768]{1,0:T(8,128)(2,1)}, bf16[96,768]{1,0:T(8,128)(2,1)S(1)}, u32[]{:S(2)}, u32[]{:S(2)}) collective-permute-start(bf16[96,768]{1,0:T(8,128)(2,1)} %param.33), channel_id=1, source_target_pairs={{0,4},{4,0},{1,5},{5,1},{2,6},{6,2},{3,7},{7,3},{8,12},{12,8},{9,1... | collective-permute-start | bytes 442376 | tf_op jit(solution)/shard_map/ppermute | solution.py:383
  3.8 16.7 %collective-permute-start.29 = (bf16[96,768]{1,0:T(8,128)(2,1)}, bf16[96,768]{1,0:T(8,128)(2,1)}, u32[]{:S(2)}, u32[]{:S(2)}) collective-permute-start(bf16[96,768]{1,0:T(8,128)(2,1)} %param.33), channel_id=1, source_target_pairs={{0,8},{8,16},{16,24},{24,0},{1,9},{9,17},{17,25},{25,1},{2,10},{10... | collective-permute-start | bytes 442376 | tf_op jit(solution)/shard_map/ppermute | solution.py:412
  5.4 18.5 %collective-permute-start = (bf16[2,64,768]{2,1,0:T(8,128)(2,1)}, bf16[2,64,768]{2,1,0:T(8,128)(2,1)S(1)}, u32[]{:S(2)}, u32[]{:S(2)}) collective-permute-start(bf16[2,64,768]{2,1,0:T(8,128)(2,1)} %param.18), channel_id=1, source_target_pairs={{0,1},{1,0},{2,3},{3,2},{4,5},{5,4},{6,7},{7,6},{8,9},{9,8},{10,11... | collective-permute-start | bytes 589832 | tf_op jit(solution)/shard_map/ppermute | solution.py:383
  10.5 7.0 %collective-permute-start.2 = (bf16[2,40,576]{2,1,0:T(8,128)(2,1)S(1)}, bf16[2,40,576]{2,1,0:T(8,128)(2,1)S(1)}, u32[]{:S(2)}, u32[]{:S(2)}) collective-permute-start(bf16[2,40,576]{2,1,0:T(8,128)(2,1)S(1)} %get-tuple-element.91), channel_id=1, source_target_pairs={{0,1},{1,0},{2,3},{3,2},{4,5},{5,4},{6,7},{7,6},{8,9},{9,8},{10,11... | collective-permute-start | bytes 276488 | tf_op jit(solution)/shard_map/ppermute | solution.py:383
  16.0 9.5 %collective-permute-start.26 = (bf16[2,64,768]{2,1,0:T(8,128)(2,1)S(1)}, bf16[2,64,768]{2,1,0:T(8,128)(2,1)S(1)}, u32[]{:S(2)}, u32[]{:S(2)}) collective-permute-start(bf16[2,64,768]{2,1,0:T(8,128)(2,1)S(1)} %multiply_convert_fusion.1), channel_id=1, source_target_pairs={{0,1},{1,0},{2,3},{3,2},{4,5},{5,4},{6,7},{7,6},{8,9},{9,8},{10,11... | collective-permute-start | bytes 589832 | tf_op jit(solution)/shard_map/ppermute | solution.py:383
  19.8 18.4 %collective-permute-start.15 = (bf16[120,768]{1,0:T(8,128)(2,1)}, bf16[120,768]{1,0:T(8,128)(2,1)}, u32[]{:S(2)}, u32[]{:S(2)}) collective-permute-start(bf16[120,768]{1,0:T(8,128)(2,1)} %get-tuple-element.97), channel_id=1, source_target_pairs={{0,4},{4,0},{1,5},{5,1},{2,6},{6,2},{3,7},{7,3},{8,12},{12,8},{9,1... | collective-permute-start | bytes 552968 | tf_op jit(solution)/shard_map/ppermute | solution.py:383
  20.5 20.4 %collective-permute-start.16 = (bf16[120,768]{1,0:T(8,128)(2,1)}, bf16[120,768]{1,0:T(8,128)(2,1)S(1)}, u32[]{:S(2)}, u32[]{:S(2)}) collective-permute-start(bf16[120,768]{1,0:T(8,128)(2,1)} %get-tuple-element.97), channel_id=1, source_target_pairs={{0,8},{8,16},{16,24},{24,0},{1,9},{9,17},{17,25},{25,1},{2,10},{10... | collective-permute-start | bytes 552968 | tf_op jit(solution)/shard_map/ppermute | solution.py:412
  22.1 8.6 %collective-permute-start.30 = (bf16[96,768]{1,0:T(8,128)(2,1)}, bf16[96,768]{1,0:T(8,128)(2,1)}, u32[]{:S(2)}, u32[]{:S(2)}) collective-permute-start(bf16[96,768]{1,0:T(8,128)(2,1)} %collective-permute-done.29), channel_id=1, source_target_pairs={{0,4},{4,0},{1,5},{5,1},{2,6},{6,2},{3,7},{7,3},{8,12},{12,8},{9,1... | collective-permute-start | bytes 442376 | tf_op jit(solution)/shard_map/ppermute | solution.py:383
  23.8 10.1 %collective-permute-start.31 = (bf16[96,768]{1,0:T(8,128)(2,1)}, bf16[96,768]{1,0:T(8,128)(2,1)S(1)}, u32[]{:S(2)}, u32[]{:S(2)}) collective-permute-start(bf16[96,768]{1,0:T(8,128)(2,1)} %collective-permute-done.29), channel_id=1, source_target_pairs={{0,8},{8,16},{16,24},{24,0},{1,9},{9,17},{17,25},{25,1},{2,10},{10... | collective-permute-start | bytes 442376 | tf_op jit(solution)/shard_map/ppermute | solution.py:412
  25.5 8.0 %collective-permute-start.4 = (bf16[112,576]{1,0:T(8,128)(2,1)S(1)}, bf16[112,576]{1,0:T(8,128)(2,1)S(1)}, u32[]{:S(2)}, u32[]{:S(2)}) collective-permute-start(bf16[112,576]{1,0:T(8,128)(2,1)S(1)} %fusion.44), channel_id=1, source_target_pairs={{0,4},{4,0},{1,5},{5,1},{2,6},{6,2},{3,7},{7,3},{8,12},{12,8},{9,1... | collective-permute-start | bytes 387080 | tf_op jit(solution)/shard_map/ppermute | solution.py:383
  33.5 27.3 %collective-permute-start.1 = (bf16[2,128,768]{2,1,0:T(8,128)(2,1)S(1)}, bf16[2,128,768]{2,1,0:T(8,128)(2,1)S(1)}, u32[]{:S(2)}, u32[]{:S(2)}) collective-permute-start(bf16[2,128,768]{2,1,0:T(8,128)(2,1)S(1)} %bitcast.432), channel_id=1, source_target_pairs={{0,2},{2,0},{1,3},{3,1},{4,6},{6,4},{5,7},{7,5},{8,10},{10,8},{9,1... | collective-permute-start | bytes 1179656 | tf_op jit(solution)/shard_map/ppermute | solution.py:383
  34.0 51.2 %collective-permute-start.27 = (bf16[2,128,768]{2,1,0:T(8,128)(2,1)S(1)}, bf16[2,128,768]{2,1,0:T(8,128)(2,1)}, u32[]{:S(2)}, u32[]{:S(2)}) collective-permute-start(bf16[2,128,768]{2,1,0:T(8,128)(2,1)S(1)} %bitcast.430), channel_id=1, source_target_pairs={{0,2},{2,0},{1,3},{3,1},{4,6},{6,4},{5,7},{7,5},{8,10},{10,8},{9,1... | collective-permute-start | bytes 1179656 | tf_op jit(solution)/shard_map/ppermute | solution.py:383
  37.6 8.2 %collective-permute-start.32 = (bf16[96,768]{1,0:T(8,128)(2,1)S(1)}, bf16[96,768]{1,0:T(8,128)(2,1)S(1)}, u32[]{:S(2)}, u32[]{:S(2)}) collective-permute-start(bf16[96,768]{1,0:T(8,128)(2,1)S(1)} %collective-permute-done.31), channel_id=1, source_target_pairs={{0,4},{4,0},{1,5},{5,1},{2,6},{6,2},{3,7},{7,3},{8,12},{12,8},{9,1... | collective-permute-start | bytes 442376 | tf_op jit(solution)/shard_map/ppermute | solution.py:383
  38.2 7.0 %collective-permute-start.6 = (bf16[112,576]{1,0:T(8,128)(2,1)S(1)}, bf16[112,576]{1,0:T(8,128)(2,1)S(1)}, u32[]{:S(2)}, u32[]{:S(2)}) collective-permute-start(bf16[112,576]{1,0:T(8,128)(2,1)S(1)} %collective-permute-done.5), channel_id=1, source_target_pairs={{0,4},{4,0},{1,5},{5,1},{2,6},{6,2},{3,7},{7,3},{8,12},{12,8},{9,1... | collective-permute-start | bytes 387080 | tf_op jit(solution)/shard_map/ppermute | solution.py:383
  40.9 8.5 %collective-permute-start.7 = (bf16[112,576]{1,0:T(8,128)(2,1)S(1)}, bf16[112,576]{1,0:T(8,128)(2,1)S(1)}, u32[]{:S(2)}, u32[]{:S(2)}) collective-permute-start(bf16[112,576]{1,0:T(8,128)(2,1)S(1)} %collective-permute-done.5), channel_id=1, source_target_pairs={{0,8},{8,16},{16,24},{24,0},{1,9},{9,17},{17,25},{25,1},{2,10},{10... | collective-permute-start | bytes 387080 | tf_op jit(solution)/shard_map/ppermute | solution.py:412
  45.1 7.1 %collective-permute-start.17 = (bf16[120,768]{1,0:T(8,128)(2,1)S(1)}, bf16[120,768]{1,0:T(8,128)(2,1)S(1)}, u32[]{:S(2)}, u32[]{:S(2)}) collective-permute-start(bf16[120,768]{1,0:T(8,128)(2,1)S(1)} %collective-permute-done.16), channel_id=1, source_target_pairs={{0,4},{4,0},{1,5},{5,1},{2,6},{6,2},{3,7},{7,3},{8,12},{12,8},{9,1... | collective-permute-start | bytes 552968 | tf_op jit(solution)/shard_map/ppermute | solution.py:383
  45.9 7.1 %collective-permute-start.33 = (bf16[96,768]{1,0:T(8,128)(2,1)S(1)}, bf16[96,768]{1,0:T(8,128)(2,1)}, u32[]{:S(2)}, u32[]{:S(2)}) collective-permute-start(bf16[96,768]{1,0:T(8,128)(2,1)S(1)} %collective-permute-done.31), channel_id=1, source_target_pairs={{0,8},{8,16},{16,24},{24,0},{1,9},{9,17},{17,25},{25,1},{2,10},{10... | collective-permute-start | bytes 442376 | tf_op jit(solution)/shard_map/ppermute | solution.py:412
  49.4 7.4 %collective-permute-start.18 = (bf16[120,768]{1,0:T(8,128)(2,1)S(1)}, bf16[120,768]{1,0:T(8,128)(2,1)}, u32[]{:S(2)}, u32[]{:S(2)}) collective-permute-start(bf16[120,768]{1,0:T(8,128)(2,1)S(1)} %collective-permute-done.16), channel_id=1, source_target_pairs={{0,8},{8,16},{16,24},{24,0},{1,9},{9,17},{17,25},{25,1},{2,10},{10... | collective-permute-start | bytes 552968 | tf_op jit(solution)/shard_map/ppermute | solution.py:412
  53.0 7.9 %collective-permute-start.9 = (bf16[112,576]{1,0:T(8,128)(2,1)S(1)}, bf16[112,576]{1,0:T(8,128)(2,1)S(1)}, u32[]{:S(2)}, u32[]{:S(2)}) collective-permute-start(bf16[112,576]{1,0:T(8,128)(2,1)S(1)} %collective-permute-done.7), channel_id=1, source_target_pairs={{0,8},{8,16},{16,24},{24,0},{1,9},{9,17},{17,25},{25,1},{2,10},{10... | collective-permute-start | bytes 387080 | tf_op jit(solution)/shard_map/ppermute | solution.py:412
  56.8 34.5 %collective-permute-start.34 = (bf16[96,768]{1,0:T(8,128)(2,1)}, bf16[96,768]{1,0:T(8,128)(2,1)}, u32[]{:S(2)}, u32[]{:S(2)}) collective-permute-start(bf16[96,768]{1,0:T(8,128)(2,1)} %collective-permute-done.33), channel_id=1, source_target_pairs={{0,4},{4,0},{1,5},{5,1},{2,6},{6,2},{3,7},{7,3},{8,12},{12,8},{9,1... | collective-permute-start | bytes 442376 | tf_op jit(solution)/shard_map/ppermute | solution.py:383
  58.9 16.6 %collective-permute-start.19 = (bf16[120,768]{1,0:T(8,128)(2,1)}, bf16[120,768]{1,0:T(8,128)(2,1)}, u32[]{:S(2)}, u32[]{:S(2)}) collective-permute-start(bf16[120,768]{1,0:T(8,128)(2,1)} %collective-permute-done.18), channel_id=1, source_target_pairs={{0,4},{4,0},{1,5},{5,1},{2,6},{6,2},{3,7},{7,3},{8,12},{12,8},{9,1... | collective-permute-start | bytes 552968 | tf_op jit(solution)/shard_map/ppermute | solution.py:383
  60.9 15.9 %collective-permute-start.20 = (bf16[120,768]{1,0:T(8,128)(2,1)}, bf16[120,768]{1,0:T(8,128)(2,1)}, u32[]{:S(2)}, u32[]{:S(2)}) collective-permute-start(bf16[120,768]{1,0:T(8,128)(2,1)} %collective-permute-done.18), channel_id=1, source_target_pairs={{0,8},{8,16},{16,24},{24,0},{1,9},{9,17},{17,25},{25,1},{2,10},{10... | collective-permute-start | bytes 552968 | tf_op jit(solution)/shard_map/ppermute | solution.py:412
  74.8 12.6 %collective-permute-start.11 = (bf16[2,2,64,192]{3,2,1,0:T(8,128)(2,1)S(1)}, bf16[2,2,64,192]{3,2,1,0:T(8,128)(2,1)S(1)}, u32[]{:S(2)}, u32[]{:S(2)}) collective-permute-start(bf16[2,2,64,192]{3,2,1,0:T(8,128)(2,1)S(1)} %get-tuple-element.84), channel_id=1, source_target_pairs={{0,1},{1,0},{2,3},{3,2},{4,5},{5,4},{6,7},{7,6},{8,9},{9,8},{10,11... | collective-permute-start | bytes 294920 | tf_op jit(solution)/shard_map/ppermute | solution.py:383
  87.6 7.0 %collective-permute-start.12 = (bf16[2,2,64,192]{3,2,1,0:T(8,128)(2,1)S(1)}, bf16[2,2,64,192]{3,2,1,0:T(8,128)(2,1)S(1)}, u32[]{:S(2)}, u32[]{:S(2)}) collective-permute-start(bf16[2,2,64,192]{3,2,1,0:T(8,128)(2,1)S(1)} %get-tuple-element.82), channel_id=1, source_target_pairs={{0,2},{2,0},{1,3},{3,1},{4,6},{6,4},{5,7},{7,5},{8,10},{10,8},{9,1... | collective-permute-start | bytes 294920 | tf_op jit(solution)/shard_map/ppermute | solution.py:383
  101.3 7.5 %collective-permute-start.24 = (bf16[2,64,768]{2,1,0:T(8,128)(2,1)}, bf16[2,64,768]{2,1,0:T(8,128)(2,1)S(1)}, u32[]{:S(2)}, u32[]{:S(2)}) collective-permute-start(bf16[2,64,768]{2,1,0:T(8,128)(2,1)} %bitcast.482), channel_id=1, source_target_pairs={{0,1},{1,0},{2,3},{3,2},{4,5},{5,4},{6,7},{7,6},{8,9},{9,8},{10,11... | collective-permute-start | bytes 589832 | tf_op jit(solution)/shard_map/ppermute | solution.py:383
  119.9 10.5 %collective-permute-start.35 = (bf16[2,2,64,768]{3,2,0,1:T(8,128)(2,1)S(1)}, bf16[2,2,64,768]{3,2,0,1:T(8,128)(2,1)S(1)}, u32[]{:S(2)}, u32[]{:S(2)}) collective-permute-start(bf16[2,2,64,768]{3,2,0,1:T(8,128)(2,1)S(1)} %bitcast.475), channel_id=1, source_target_pairs={{0,2},{2,0},{1,3},{3,1},{4,6},{6,4},{5,7},{7,5},{8,10},{10,8},{9,1... | collective-permute-start | bytes 1179656 | tf_op jit(solution)/shard_map/ppermute | solution.py:383
  124.0 21.4 %collective-permute-start.60 = (bf16[4,96,768]{2,1,0:T(8,128)(2,1)}, bf16[4,96,768]{2,1,0:T(8,128)(2,1)}, u32[]{:S(2)}, u32[]{:S(2)}) collective-permute-start(bf16[4,96,768]{2,1,0:T(8,128)(2,1)} %dynamic-slice_bitcast_fusion.1), channel_id=1, source_target_pairs={{0,4},{4,0},{1,5},{5,1},{2,6},{6,2},{3,7},{7,3},{8,12},{12,8},{9,1... | collective-permute-start | bytes 1769480 | tf_op jit(solution)/shard_map/ppermute | solution.py:383
  126.7 25.8 %collective-permute-start.66 = (bf16[4,96,768]{2,1,0:T(8,128)(2,1)}, bf16[4,96,768]{2,1,0:T(8,128)(2,1)}, u32[]{:S(2)}, u32[]{:S(2)}) collective-permute-start(bf16[4,96,768]{2,1,0:T(8,128)(2,1)} %dynamic-slice_bitcast_fusion), channel_id=1, source_target_pairs={{0,4},{4,0},{1,5},{5,1},{2,6},{6,2},{3,7},{7,3},{8,12},{12,8},{9,1... | collective-permute-start | bytes 1769480 | tf_op jit(solution)/shard_map/ppermute | solution.py:383
  129.0 7.8 %collective-permute-start.38 = (bf16[2,64,768]{2,1,0:T(8,128)(2,1)S(1)}, bf16[2,64,768]{2,1,0:T(8,128)(2,1)S(1)}, u32[]{:S(2)}, u32[]{:S(2)}) collective-permute-start(bf16[2,64,768]{2,1,0:T(8,128)(2,1)S(1)} %fusion.40), channel_id=1, source_target_pairs={{0,1},{1,0},{2,3},{3,2},{4,5},{5,4},{6,7},{7,6},{8,9},{9,8},{10,11... | collective-permute-start | bytes 589832 | tf_op jit(solution)/shard_map/ppermute | solution.py:383
  131.3 15.2 %collective-permute-start.36 = (bf16[2,64,768]{2,1,0:T(8,128)(2,1)}, bf16[2,64,768]{2,1,0:T(8,128)(2,1)S(1)}, u32[]{:S(2)}, u32[]{:S(2)}) collective-permute-start(bf16[2,64,768]{2,1,0:T(8,128)(2,1)} %fusion.39), channel_id=1, source_target_pairs={{0,1},{1,0},{2,3},{3,2},{4,5},{5,4},{6,7},{7,6},{8,9},{9,8},{10,11... | collective-permute-start | bytes 589832 | tf_op jit(solution)/shard_map/ppermute | solution.py:383
  142.5 11.1 %collective-permute-start.39 = (bf16[2,2,64,192]{3,2,1,0:T(8,128)(2,1)S(1)}, bf16[2,2,64,192]{3,2,1,0:T(8,128)(2,1)S(1)}, u32[]{:S(2)}, u32[]{:S(2)}) collective-permute-start(bf16[2,2,64,192]{3,2,1,0:T(8,128)(2,1)S(1)} %bitcast.499), channel_id=1, source_target_pairs={{0,1},{1,0},{2,3},{3,2},{4,5},{5,4},{6,7},{7,6},{8,9},{9,8},{10,11... | collective-permute-start | bytes 294920 | tf_op jit(solution)/shard_map/ppermute | solution.py:383
  145.4 50.3 %collective-permute-start.54 = (bf16[8,2,24,768]{3,2,1,0:T(8,128)(2,1)}, bf16[8,2,24,768]{3,2,1,0:T(8,128)(2,1)}, u32[]{:S(2)}, u32[]{:S(2)}) collective-permute-start(bf16[8,2,24,768]{3,2,1,0:T(8,128)(2,1)} %dynamic-slice_bitcast_fusion.2), channel_id=1, source_target_pairs={{0,2},{2,0},{1,3},{3,1},{4,6},{6,4},{5,7},{7,5},{8,10},{10,8},{9,1... | collective-permute-start | bytes 1769480 | tf_op jit(solution)/shard_map/ppermute | solution.py:383
  146.4 8.2 %collective-permute-start.61 = (bf16[96,768]{1,0:T(8,128)(2,1)S(1)}, bf16[96,768]{1,0:T(8,128)(2,1)S(1)}, u32[]{:S(2)}, u32[]{:S(2)}) collective-permute-start(bf16[96,768]{1,0:T(8,128)(2,1)S(1)} %fusion.23), channel_id=1, source_target_pairs={{0,8},{8,16},{16,24},{24,0},{1,9},{9,17},{17,25},{25,1},{2,10},{10... | collective-permute-start | bytes 442376 | tf_op jit(solution)/shard_map/ppermute | solution.py:434
  153.4 7.2 %collective-permute-start.67 = (bf16[96,768]{1,0:T(8,128)(2,1)S(1)}, bf16[96,768]{1,0:T(8,128)(2,1)S(1)}, u32[]{:S(2)}, u32[]{:S(2)}) collective-permute-start(bf16[96,768]{1,0:T(8,128)(2,1)S(1)} %fusion.16), channel_id=1, source_target_pairs={{0,8},{8,16},{16,24},{24,0},{1,9},{9,17},{17,25},{25,1},{2,10},{10... | collective-permute-start | bytes 442376 | tf_op jit(solution)/shard_map/ppermute | solution.py:434
  153.6 8.6 %collective-permute-start.40 = (bf16[2,2,64,192]{3,2,1,0:T(8,128)(2,1)S(1)}, bf16[2,2,64,192]{3,2,1,0:T(8,128)(2,1)S(1)}, u32[]{:S(2)}, u32[]{:S(2)}) collective-permute-start(bf16[2,2,64,192]{3,2,1,0:T(8,128)(2,1)S(1)} %get-tuple-element.78), channel_id=1, source_target_pairs={{0,2},{2,0},{1,3},{3,1},{4,6},{6,4},{5,7},{7,5},{8,10},{10,8},{9,1... | collective-permute-start | bytes 294920 | tf_op jit(solution)/shard_map/ppermute | solution.py:383
  156.3 20.9 %collective-permute-start.62 = (bf16[96,768]{1,0:T(8,128)(2,1)}, bf16[96,768]{1,0:T(8,128)(2,1)}, u32[]{:S(2)}, u32[]{:S(2)}) collective-permute-start(bf16[96,768]{1,0:T(8,128)(2,1)} %fusion.22), channel_id=1, source_target_pairs={{0,8},{8,16},{16,24},{24,0},{1,9},{9,17},{17,25},{25,1},{2,10},{10... | collective-permute-start | bytes 442376 | tf_op jit(solution)/shard_map/ppermute | solution.py:434
  162.3 16.5 %collective-permute-start.68 = (bf16[96,768]{1,0:T(8,128)(2,1)}, bf16[96,768]{1,0:T(8,128)(2,1)}, u32[]{:S(2)}, u32[]{:S(2)}) collective-permute-start(bf16[96,768]{1,0:T(8,128)(2,1)} %fusion.15), channel_id=1, source_target_pairs={{0,8},{8,16},{16,24},{24,0},{1,9},{9,17},{17,25},{25,1},{2,10},{10... | collective-permute-start | bytes 442376 | tf_op jit(solution)/shard_map/ppermute | solution.py:434
  172.4 20.6 %collective-permute-start.41 = (bf16[2,2,64,768]{3,2,0,1:T(8,128)(2,1)}, bf16[2,2,64,768]{3,2,0,1:T(8,128)(2,1)}, u32[]{:S(2)}, u32[]{:S(2)}) collective-permute-start(bf16[2,2,64,768]{3,2,0,1:T(8,128)(2,1)} %bitcast.404), channel_id=1, source_target_pairs={{0,2},{2,0},{1,3},{3,1},{4,6},{6,4},{5,7},{7,5},{8,10},{10,8},{9,1... | collective-permute-start | bytes 1179656 | tf_op jit(solution)/shard_map/ppermute | solution.py:383
  176.0 20.8 %collective-permute-start.48 = (bf16[4,96,576]{2,1,0:T(8,128)(2,1)}, bf16[4,96,576]{2,1,0:T(8,128)(2,1)}, u32[]{:S(2)}, u32[]{:S(2)}) collective-permute-start(bf16[4,96,576]{2,1,0:T(8,128)(2,1)} %dynamic-slice_bitcast_fusion.3), channel_id=1, source_target_pairs={{0,4},{4,0},{1,5},{5,1},{2,6},{6,2},{3,7},{7,3},{8,12},{12,8},{9,1... | collective-permute-start | bytes 1327112 | tf_op jit(solution)/shard_map/ppermute | solution.py:383
  178.4 8.6 %collective-permute-start.63 = (bf16[96,768]{1,0:T(8,128)(2,1)S(1)}, bf16[96,768]{1,0:T(8,128)(2,1)S(1)}, u32[]{:S(2)}, u32[]{:S(2)}) collective-permute-start(bf16[96,768]{1,0:T(8,128)(2,1)S(1)} %fusion.20), channel_id=1, source_target_pairs={{0,8},{8,16},{16,24},{24,0},{1,9},{9,17},{17,25},{25,1},{2,10},{10... | collective-permute-start | bytes 442376 | tf_op jit(solution)/shard_map/ppermute | solution.py:434
  179.9 9.8 %collective-permute-start.69 = (bf16[96,768]{1,0:T(8,128)(2,1)S(1)}, bf16[96,768]{1,0:T(8,128)(2,1)S(1)}, u32[]{:S(2)}, u32[]{:S(2)}) collective-permute-start(bf16[96,768]{1,0:T(8,128)(2,1)S(1)} %fusion.13), channel_id=1, source_target_pairs={{0,8},{8,16},{16,24},{24,0},{1,9},{9,17},{17,25},{25,1},{2,10},{10... | collective-permute-start | bytes 442376 | tf_op jit(solution)/shard_map/ppermute | solution.py:434
  194.2 11.4 %collective-permute-start.42 = (bf16[2,64,768]{2,1,0:T(8,128)(2,1)S(1)}, bf16[2,64,768]{2,1,0:T(8,128)(2,1)S(1)}, u32[]{:S(2)}, u32[]{:S(2)}) collective-permute-start(bf16[2,64,768]{2,1,0:T(8,128)(2,1)S(1)} %fusion.41), channel_id=1, source_target_pairs={{0,1},{1,0},{2,3},{3,2},{4,5},{5,4},{6,7},{7,6},{8,9},{9,8},{10,11... | collective-permute-start | bytes 589832 | tf_op jit(solution)/shard_map/ppermute | solution.py:383
  198.0 15.3 %collective-permute-start.55 = (bf16[8,24,768]{2,1,0:T(8,128)(2,1)S(1)}, bf16[8,24,768]{2,1,0:T(8,128)(2,1)}, u32[]{:S(2)}, u32[]{:S(2)}) collective-permute-start(bf16[8,24,768]{2,1,0:T(8,128)(2,1)S(1)} %fusion.2), channel_id=1, source_target_pairs={{0,1},{1,0},{2,3},{3,2},{4,5},{5,4},{6,7},{7,6},{8,9},{9,8},{10,11... | collective-permute-start | bytes 884744 | tf_op jit(solution)/shard_map/ppermute | solution.py:383
  209.8 12.5 %collective-permute-start.65 = (bf16[2,24,8,96]{3,2,1,0:T(8,128)(2,1)S(1)}, bf16[2,24,8,96]{3,2,1,0:T(8,128)(2,1)S(1)}, u32[]{:S(2)}, u32[]{:S(2)}) collective-permute-start(bf16[2,24,8,96]{3,2,1,0:T(8,128)(2,1)S(1)} %get-tuple-element.93), channel_id=1, source_target_pairs={{0,2},{2,0},{1,3},{3,1},{4,6},{6,4},{5,7},{7,5},{8,10},{10,8},{9,1... | collective-permute-start | bytes 221192 | tf_op jit(solution)/shard_map/ppermute | solution.py:383
  214.3 10.9 %collective-permute-start.56 = (bf16[4,24,768]{2,1,0:T(8,128)(2,1)S(1)}, bf16[4,24,768]{2,1,0:T(8,128)(2,1)S(1)}, u32[]{:S(2)}, u32[]{:S(2)}) collective-permute-start(bf16[4,24,768]{2,1,0:T(8,128)(2,1)S(1)} %dynamic-slice_bitcast_fusion.4), channel_id=1, source_target_pairs={{0,4},{4,0},{1,5},{5,1},{2,6},{6,2},{3,7},{7,3},{8,12},{12,8},{9,1... | collective-permute-start | bytes 442376 | tf_op jit(solution)/shard_map/ppermute | solution.py:383
  215.9 7.9 %collective-permute-start.45 = (f32[24,768]{1,0:T(8,128)S(1)}, f32[24,768]{1,0:T(8,128)S(1)}, u32[]{:S(2)}, u32[]{:S(2)}) collective-permute-start(f32[24,768]{1,0:T(8,128)S(1)} %add.468), channel_id=1, source_target_pairs={{0,4},{4,0},{1,5},{5,1},{2,6},{6,2},{3,7},{7,3},{8,12},{12,8},{9,1... | collective-permute-start | bytes 221192 | tf_op jit(solution)/shard_map/ppermute | solution.py:383
  223.8 7.4 %collective-permute-start.46 = (f32[24,768]{1,0:T(8,128)S(1)}, f32[24,768]{1,0:T(8,128)S(1)}, u32[]{:S(2)}, u32[]{:S(2)}) collective-permute-start(f32[24,768]{1,0:T(8,128)S(1)} %add.469), channel_id=1, source_target_pairs={{0,8},{8,0},{16,24},{24,16},{1,9},{9,1},{17,25},{25,17},{2,10},{10... | collective-permute-start | bytes 221192 | tf_op jit(solution)/shard_map/ppermute | solution.py:659
  231.2 12.2 %collective-permute-start.47 = (f32[24,768]{1,0:T(8,128)S(1)}, f32[24,768]{1,0:T(8,128)S(1)}, u32[]{:S(2)}, u32[]{:S(2)}) collective-permute-start(f32[24,768]{1,0:T(8,128)S(1)} %add.470), channel_id=1, source_target_pairs={{0,16},{8,24},{16,0},{24,8},{1,17},{9,25},{17,1},{25,9},{2,18},{10... | collective-permute-start | bytes 221192 | tf_op jit(solution)/shard_map/ppermute | solution.py:659
  (64 other events, 377.8 us)

commit v2 on v0

--- a/solution.py
+++ b/solution.py
@@ -1,8 +1,12 @@
+import functools
 import math
 
 import jax
 import jax.numpy as jnp
 from jax import lax
+from jax.experimental import pallas as pl
+from jax.experimental.pallas import tpu as pltpu
+from jax.sharding import Mesh
 from jax.sharding import PartitionSpec as P
 
 HEADS = 12
@@ -40,7 +44,7 @@
     return jnp.dot(left, right, preferred_element_type=jnp.float32)
 
 
-def on_device(
+def on_device_gathered(
     inputs,
     micro_live,
     ln1_gain,
@@ -217,46 +221,648 @@
     )
 
 
+F32 = jnp.float32
+BF16 = jnp.bfloat16
+SCALE = 1.0 / math.sqrt(HD)
+SWAP = ((0, 1), (1, 0))
+VMEM_LIMIT = 56 * 1024 * 1024
+G1, C1, BQ, BV, BO, G2, C2, BF2, BF1 = range(9)
+
+
+def nt_dot(left, right):
+    return lax.dot_general(left, right, (((1,), (1,)), ((), ())), preferred_element_type=F32)
+
+
+def tn_dot(left, right):
+    return lax.dot_general(left, right, (((0,), (0,)), ((), ())), preferred_element_type=F32)
+
+
+def row_of(named, n):
+    return named[n : n + 1, :].astype(F32)
+
+
+def head_masks(rows, width):
+    lanes = lax.broadcasted_iota(jnp.int32, (rows, width), 1)
+    return [
+        jnp.where((lanes >= h * HD) & (lanes < (h + 1) * HD), 1.0, 0.0).astype(F32)
+        for h in range(width // HD)
+    ]
+
+
+def quarter_of(row, me, part):
+    total = None
+    for t in range(4):
+        piece = jnp.where(me == t, 1.0, 0.0).astype(F32) * row[:, t * part : (t + 1) * part]
+        total = piece if total is None else total + piece
+    return total
+
+
+def pack_columns(spot, w_q, w_k, w_v, vectors, own, along_y, along_c):
+    me = spot[4]
+    part = own.shape[1] // 3
+    mats = [r[...].astype(F32) for r in (w_q, w_k, w_v)]
+    pads = vectors[...].astype(F32)
+
+    def piece(t):
+        columns = jnp.concatenate([m[:, t * part : (t + 1) * part] for m in mats], axis=1)
+        return jnp.concatenate([columns, pads], axis=0).astype(BF16)
+
+    for t in range(4):
+        value = piece(t)
+        rel = t ^ me
+
+        @pl.when(rel == 0)
+        def _():
+            own[...] = value
+
+        @pl.when(rel == 2)
+        def _():
+            along_c[...] = value
+
+        @pl.when(rel == 1)
+        def _():
+            along_y[0] = value
+
+        @pl.when(rel == 3)
+        def _():
+            along_y[1] = value
+
+
+def clip_rows(base, s, count, rows):
+    return (
+        pl.ds(pl.multiple_of(base + s * count, count), count),
+        pl.ds(pl.multiple_of(base + rows + s * count, count), count),
+    )
+
+
+def attention_forward(
+    spot, x0, x1, x2, x3, named, weight, h1_ref, q_ref, k_ref, v_ref, probs_ref, own, along_y, along_c, ctx
+):
+    slots, count, width = x0.shape
+    rows = slots * count
+    part = q_ref.shape[1]
+    names = named[...]
+    gain, shift = row_of(names, G1), row_of(names, C1)
+    for n, x in enumerate((x0, x1, x2, x3)):
+        h1, _, _ = layer_norm(x[...].reshape(rows, width).astype(F32), gain, shift)
+        h1_ref[n * rows : (n + 1) * rows, :] = h1.astype(BF16)
+    me = spot[4]
+    qkv = tdot(h1_ref[...], weight[...])
+    q_ref[...] = (qkv[:, :part] + quarter_of(row_of(names, BQ), me, part)).astype(BF16)
+    k_ref[...] = qkv[:, part : 2 * part].astype(BF16)
+    v_ref[...] = (qkv[:, 2 * part :] + quarter_of(row_of(names, BV), me, part)).astype(BF16)
+    masks32 = head_masks(2 * count, part)
+    masks = [m.astype(BF16) for m in masks32]
+
+    def one(pair, carry):
+        base = pair * 2 * rows
+        for s in range(slots):
+            low, high = clip_rows(base, s, count, rows)
+            qs, ks, vs = [
+                jnp.concatenate([r[low, :], r[high, :]], axis=0) for r in (q_ref, k_ref, v_ref)
+            ]
+            total = None
+            for h, (mask, mask32) in enumerate(zip(masks, masks32)):
+                scores = nt_dot(qs * mask, ks) * SCALE
+                peak = jnp.max(scores, axis=-1, keepdims=True)
+                lse = peak + jnp.log(jnp.sum(jnp.exp(scores - peak), axis=-1, keepdims=True))
+                probs = jnp.exp(scores - lse)
+                probs_ref[(pair * slots + s) * len(masks) + h] = probs
+                term = tdot(probs.astype(BF16), vs) * mask32
+                total = term if total is None else total + term
+            totalb = total.astype(BF16)
+            ctx[low, :] = totalb[:count]
+            ctx[high, :] = totalb[count:]
+        return carry
+
+    lax.fori_loop(0, 2, one, 0)
+    own[...] = ctx[0:rows, :]
+    along_y[0] = ctx[rows : 2 * rows, :]
+    along_c[...] = ctx[2 * rows : 3 * rows, :]
+    along_y[1] = ctx[3 * rows : 4 * rows, :]
+
+
+def attention_backward(
+    spot, d0, d1, d2, d3, q_ref, k_ref, v_ref, probs_ref, weight, h1_ref,
+    dh_own, dh_c, bq_ref, bv_ref, keep, send_far, send_near, dctx, grads
+):
+    rows = d0.shape[0]
+    part = q_ref.shape[1]
+    count = probs_ref.shape[1] // 2
+    slots = rows // count
+    for n, d in enumerate((d0, d1, d2, d3)):
+        dctx[n * rows : (n + 1) * rows, :] = d[...]
+    masks32 = head_masks(2 * count, part)
+    masks = [m.astype(BF16) for m in masks32]
+    bq_ref[...] = jnp.zeros(bq_ref.shape, F32)
+    bv_ref[...] = jnp.zeros(bv_ref.shape, F32)
+
+    def one(pair, carry):
+        base = pair * 2 * rows
+        for s in range(slots):
+            low, high = clip_rows(base, s, count, rows)
+            ds_, qs, ks, vs = [
+                jnp.concatenate([r[low, :], r[high, :]], axis=0)
+                for r in (dctx, q_ref, k_ref, v_ref)
+            ]
+            dq = dk = dv = None
+            for h, (mask, mask32) in enumerate(zip(masks, masks32)):
+                p = probs_ref[(pair * slots + s) * len(masks) + h]
+                dprob = nt_dot(ds_ * mask, vs)
+                delta = jnp.sum(p * dprob, axis=-1, keepdims=True)
+                dsb = (p * (dprob - delta) * SCALE).astype(BF16)
+                tq = tdot(dsb, ks) * mask32
+                tk = tn_dot(dsb, qs) * mask32
+                tv = tn_dot(p.astype(BF16), ds_) * mask32
+                dq = tq if dq is None else dq + tq
+                dk = tk if dk is None else dk + tk
+                dv = tv if dv is None else dv + tv
+            bq_ref[...] += jnp.sum(dq, axis=0, keepdims=True)
+            bv_ref[...] += jnp.sum(dv, axis=0, keepdims=True)
+            all_three = jnp.concatenate([dq, dk, dv], axis=1).astype(BF16)
+            grads[low, :] = all_three[:count]
+            grads[high, :] = all_three[count:]
+        return carry
+
+    lax.fori_loop(0, 2, one, 0)
+    place_blocks(spot, tn_dot(h1_ref[...], grads[...]), keep, (send_near, send_far))
+    dh1 = nt_dot(grads[...], weight[...]).astype(BF16)
+    for n in range(2):
+        dh_own[n] = dh1[n * rows : (n + 1) * rows]
+        dh_c[n] = dh1[(2 + n) * rows : (3 + n) * rows]
+
+
+def place_blocks(spot, grad, keep, sends):
+    z, x = spot[0], spot[1]
+    size = keep.shape[1]
+    held = keep.shape[0] // len(sends)
+    for zz in range(keep.shape[0]):
+        pair = [grad[(2 * zz + n) * size : (2 * zz + n + 1) * size] for n in range(2)]
+        far = zz ^ z
+        first = x == 0
+        keep[far] = jnp.where(first, pair[0], pair[1]).astype(BF16)
+        other = jnp.where(first, pair[1], pair[0]).astype(BF16)
+        for n, ref in enumerate(sends):
+            if len(sends) == 1:
+                ref[far] = other
+            else:
+
+                @pl.when((far >= n * held) & (far < (n + 1) * held))
+                def _():
+                    ref[far - n * held] = other
+
+
+def out_projection(spot, x, c0, c1, c2, c3, weight, named, mid_ref, h2_ref):
+    me = spot[4]
+    names = named[...]
+    total = x[...].astype(F32) + row_of(names, BO)
+    for n, piece in enumerate((c0, c1, c2, c3)):
+        total = total + tdot(piece[...], weight[me ^ n])
+    mid_ref[...] = total
+    h2, _, _ = layer_norm(total, row_of(names, G2), row_of(names, C2))
+    h2_ref[...] = h2.astype(BF16)
+
+
+def feed_forward(
+    spot, a0, a1, a2, a3, g0, g1, g2, g3, first, second, named,
+    h2_ref, gy_ref, act_ref, dpre_ref, dh_own, dh_c, sum_ref
+):
+    rows = a0.shape[0]
+    for n, (a, g) in enumerate(((a0, g0), (a1, g1), (a2, g2), (a3, g3))):
+        h2_ref[n * rows : (n + 1) * rows, :] = a[...]
+        gy_ref[n * rows : (n + 1) * rows, :] = g[...]
+    bias = row_of(named[...], BF1)
+    sum_ref[...] = jnp.zeros(sum_ref.shape, F32)
+
+    def one(pair, carry):
+        block = pl.ds(pl.multiple_of(pair * 2 * rows, 2 * rows), 2 * rows)
+        pre = tdot(h2_ref[block, :], first[...]) + bias
+        phi = 0.5 * (1.0 + lax.erf(pre * 0.7071067811865476))
+        act_ref[block, :] = (pre * phi).astype(BF16)
+        slope = phi + pre * jnp.exp(-0.5 * pre * pre) * 0.3989422804014327
+        dpre = nt_dot(gy_ref[block, :], second[...]) * slope
+        dpreb = dpre.astype(BF16)
+        dpre_ref[block, :] = dpreb
+        sum_ref[...] += jnp.sum(dpre, axis=0, keepdims=True)
+        dh2 = nt_dot(dpreb, first[...]).astype(BF16)
+
+        @pl.when(pair == 0)
+        def _():
+            dh_own[0] = dh2[:rows]
+            dh_own[1] = dh2[rows:]
+
+        @pl.when(pair == 1)
+        def _():
+            dh_c[0] = dh2[:rows]
+            dh_c[1] = dh2[rows:]
+
+        return carry
+
+    lax.fori_loop(0, 2, one, 0)
+
+
+def weight_gradient(spot, left, right, keep, send):
+    place_blocks(spot, tn_dot(left[...], right[...]), keep, (send,))
+
+
+def out_rows_part(spot, act, second, own, along_c):
+    rows = own.shape[1]
+    value = tdot(act[...], second[...]).astype(BF16)
+    for n in range(2):
+        own[n] = value[n * rows : (n + 1) * rows]
+        along_c[n] = value[(2 + n) * rows : (3 + n) * rows]
+
+
+def middle_backward(
+    spot, d0, d1, d2, mid_ref, gy_ref, weight, named, dmid_ref, dmidb_ref, own, along_y, along_c, sums
+):
+    me = spot[4]
+    gain = row_of(named[...], G2)
+    gy = gy_ref[...].astype(F32)
+    dh2 = d0[0].astype(F32) + d1[0].astype(F32) + d2[...].astype(F32)
+    _, normed, inv = layer_norm(mid_ref[...], gain, gain)
+    dmid = gy + norm_back(dh2, normed, inv, gain)
+    dmidb = dmid.astype(BF16)
+    dmid_ref[...] = dmid
+    dmidb_ref[...] = dmidb
+    parts = [nt_dot(dmidb, weight[me ^ n]).astype(BF16) for n in range(4)]
+    own[...] = parts[0]
+    along_y[0] = parts[1]
+    along_c[...] = parts[2]
+    along_y[1] = parts[3]
+    for n, value in enumerate((dmid, dh2 * normed, dh2, gy)):
+        sums[n : n + 1, :] = jnp.sum(value, axis=0, keepdims=True)
+    sums[4:8, :] = jnp.zeros((4, gain.shape[1]), F32)
+
+
+def out_gradient(spot, c0, c1, c2, c3, dmidb, own, along_c, held):
+    z, x, c, y, me = [spot[n] for n in range(5)]
+    size = held.shape[1]
+    for n, piece in enumerate((c0, c1, c2, c3)):
+        value = tn_dot(piece[...], dmidb[...])
+        for b in range(8):
+            held[b] = value[b * size : (b + 1) * size]
+        far = (me ^ n) ^ z
+        for cc, ref in enumerate((own, along_c)):
+            for yy in range(2):
+                pair = [held[4 * (x ^ xx) + 2 * (c ^ cc) + (y ^ yy)] for xx in range(2)]
+                ref[yy, far] = jnp.concatenate(pair, axis=0).astype(BF16)
+
+
+def input_backward(spot, d0, d1, d2, dmid, x, named, grad_ref, sums):
+    gain = row_of(named[...], G1)
+    dh1 = d0[0].astype(F32) + d1[0].astype(F32) + d2[...].astype(F32)
+    _, normed, inv = layer_norm(x[...].astype(F32), gain, gain)
+    grad_ref[...] = dmid[...] + norm_back(dh1, normed, inv, gain)
+    sums[0:1, :] = jnp.sum(dh1 * normed, axis=0, keepdims=True)
+    sums[1:2, :] = jnp.sum(dh1, axis=0, keepdims=True)
+    sums[2:8, :] = jnp.zeros((6, gain.shape[1]), F32)
+
+
+def run_kernel(body, spot, ins, outs, scratch, flops):
+    moved = sum(a.size * a.dtype.itemsize for a in ins)
+    moved += sum(math.prod(s) * jnp.dtype(d).itemsize for s, d in outs)
+    return pl.pallas_call(
+        body,
+        in_specs=[pl.BlockSpec(memory_space=pltpu.SMEM)]
+        + [pl.BlockSpec(memory_space=pltpu.VMEM)] * len(ins),
+        out_specs=[pl.BlockSpec(memory_space=pltpu.VMEM)] * len(outs),
+        out_shape=[jax.ShapeDtypeStruct(s, d) for s, d in outs],
+        scratch_shapes=[pltpu.VMEM(s, d) for s, d in scratch],
+        compiler_params=pltpu.CompilerParams(vmem_limit_bytes=VMEM_LIMIT),
+        cost_estimate=pl.CostEstimate(flops=flops, bytes_accessed=moved, transcendentals=0),
+        name=body.__name__,
+    )(spot, *ins)
+
+
+def swap(value, axis):
+    return lax.ppermute(value, axis, SWAP)
+
+
+def after(value, *others):
+    return lax.optimization_barrier((value, *others))[0]
+
+
+def pick(value, index, axis=0):
+    return lax.dynamic_index_in_dim(value, index, axis, keepdims=False)
+
+
+def ordered(own, other, index, axis):
+    return jnp.where(index == 0, jnp.stack([own, other], axis), jnp.stack([other, own], axis))
+
+
+def trade_pair(value, axis_name, index, axis):
+    other = swap(pick(value, 1 - index, axis), axis_name)
+    return ordered(pick(value, index, axis), other, index, axis)
+
+
+def share_rows(value):
+    over_y = swap(value, "y")
+    return value, over_y, swap(value, "c"), swap(over_y, "c")
+
+
+def trade_rows(own, along_y, along_c):
+    over_y = swap(along_y, "y")
+    return own, over_y[0], swap(along_c, "c"), swap(over_y[1], "c")
+
+
+def sum_rows(own, along_c):
+    over_c = swap(along_c, "c")
+    other = (own[1].astype(F32) + over_c[1].astype(F32)).astype(BF16)
+    return own, over_c, swap(other, "y")
+
+
+def far_in_z(value, distance, ring):
+    return lax.ppermute(value, "z", tuple((i, i ^ distance) for i in range(ring)))
+
+
+def wide_gather(block, ring, place, sizes):
+    z, x = place
+    starts = [sum(sizes[:n]) for n in range(len(sizes))]
+    outs = [jnp.zeros((2 * ring, n, block.shape[1]), block.dtype) for n in sizes]
+    blocks = [block] + [far_in_z(block, d, ring) for d in range(1, ring)]
+    for d, held in enumerate(blocks):
+        for side, value in ((x, held), (1 - x, swap(held, "x"))):
+            at = 2 * (z ^ d) + side
+            for n, (start, size) in enumerate(zip(starts, sizes)):
+                outs[n] = lax.dynamic_update_slice(
+                    outs[n], value[None, start : start + size], (at, 0, 0)
+                )
+    return outs, blocks
+
+
+def wide_sum(keep, others, ring):
+    half = [keep[d].astype(F32) + others[d].astype(F32) for d in range(ring)]
+    total = half[0]
+    for d in range(ring - 1, 0, -1):
+        total = total + far_in_z(half[d].astype(BF16), d, ring).astype(F32)
+    return total
+
+
+def on_device_split(
+    ring,
+    inputs,
+    micro_live,
+    ln1_gain,
+    ln1_shift,
+    w_q,
+    b_q,
+    w_k,
+    w_v,
+    b_v,
+    w_o,
+    b_o,
+    ln2_gain,
+    ln2_shift,
+    w_fc1,
+    b_fc1,
+    w_fc2,
+    b_fc2,
+    grad_out,
+):
+    z, x, c, y = (lax.axis_index(a) for a in ("z", "x", "c", "y"))
+    place = (z, x)
+    me = 2 * c + y
+    spot = jnp.stack([z, x, c, y, me]).astype(jnp.int32)
+    slots, count, width = inputs.shape
+    rows = slots * count
+    shard = w_q.shape[0]
+    units = w_fc2.shape[0]
+    groups = 2 * ring
+    part = width // 4
+    wide = w_fc1.shape[1] // 4
+    all_slots, frames = 2 * slots, 2 * count
+    all_rows = all_slots * frames
+    heads = part // HD
+
+    def trade_four(value):
+        cut = value.reshape(2, 2, *value.shape[1:])
+        return trade_pair(trade_pair(cut, "y", y, 1), "c", c, 0).reshape(value.shape)
+
+    vector_rows = jnp.stack([ln1_gain, ln1_shift, b_q, b_v, b_o, ln2_gain, ln2_shift, b_fc2])
+    vector_rows = jnp.pad(vector_rows, ((0, 0), (0, 3 * part - shard)))
+    piece = ((shard + 8, 3 * part), BF16)
+    own, along_y, along_c = run_kernel(
+        pack_columns,
+        spot,
+        (w_q, w_k, w_v, vector_rows),
+        [piece, ((2, *piece[0]), BF16), piece],
+        [],
+        0,
+    )
+    pieces = trade_rows(own, along_y, along_c)
+    first = jnp.zeros((4, *piece[0]), BF16)
+    for n, value in enumerate(pieces):
+        first = lax.dynamic_update_slice(first, value[None], (me ^ n, 0, 0))
+    vectors = first[:, shard:, :shard].transpose(1, 0, 2).reshape(8, 4 * shard)
+    vectors = jnp.pad(vectors, ((0, 0), (0, 3 * part - 4 * shard)))
+    units_row = jnp.pad(b_fc1.reshape(1, units), ((0, 7), (0, 3 * part - units)))
+    block = jnp.concatenate([first[:, :shard].reshape(4 * shard, 3 * part), vectors, units_row])
+    x_all = share_rows(inputs)
+    (w_qkv, vectors), arrived = wide_gather(block, ring, place, (4 * shard, 16))
+    w_qkv = w_qkv.reshape(width, 3 * part)
+    named = vectors[:, :, : 4 * shard].transpose(1, 0, 2).reshape(16, width)
+
+    wo_block = after(w_o, arrived[1])
+    (wo,), _ = wide_gather(wo_block, ring, place, (shard,))
+    wo = ordered(wo, swap(wo, "y"), y, 1)
+    wo = ordered(wo, swap(wo, "c"), c, 1).reshape(4, part, width)
+    columns = w_fc1.reshape(shard, groups, 4, units).transpose(2, 0, 1, 3).reshape(4, shard, wide)
+    block = trade_four(after(columns, pieces[1])).reshape(4 * shard, wide)
+    block = after(jnp.concatenate([block, w_fc2]), arrived[ring - 1])
+    (wf1, wf2), _ = wide_gather(block, ring, place, (4 * shard, units))
+    wf1 = wf1.reshape(width, wide)
+    wf2 = wf2.reshape(wide, width)
+    live = micro_live.astype(F32)[:, None, None]
+    gy_own = (live * grad_out.astype(F32)).astype(BF16).reshape(rows, width)
+    gy_all = share_rows(after(gy_own, x_all[1]))
+
+    row_part = ((all_rows, part), BF16)
+    mine = [((rows, part), BF16), ((2, rows, part), BF16), ((rows, part), BF16)]
+    h1b, q, k, v, probs, *ctx = run_kernel(
+        attention_forward,
+        spot,
+        (*x_all, named, w_qkv),
+        [
+            ((all_rows, width), BF16),
+            row_part,
+            row_part,
+            row_part,
+            ((all_slots * heads, frames, frames), F32),
+            *mine,
+        ],
+        [row_part],
+        2 * all_rows * part * (3 * width + 2 * frames),
+    )
+    ctx = trade_rows(*ctx)
+    x_own = inputs.reshape(rows, width)
+    mid, h2_own = run_kernel(
+        out_projection,
+        spot,
+        (x_own, *ctx, wo, named),
+        [((rows, width), F32), ((rows, width), BF16)],
+        [],
+        2 * rows * width * width,
+    )
+    pair_rows = ((2, rows, width), BF16)
+    h2_all, gy_rows, act, dpreb, dh2_own, dh2_c, dpre_sum = run_kernel(
+        feed_forward,
+        spot,
+        (*share_rows(h2_own), *gy_all, wf1, wf2, named),
+        [
+            ((all_rows, width), BF16),
+            ((all_rows, width), BF16),
+            ((all_rows, wide), BF16),
+            ((all_rows, wide), BF16),
+            pair_rows,
+            pair_rows,
+            ((1, wide), F32),
+        ],
+        [],
+        6 * all_rows * width * wide,
+    )
+
+    dh2 = sum_rows(dh2_own, dh2_c)
+
+    def weight_grad(left, right, size):
+        shape = ((ring, size, right.shape[1]), BF16)
+        flops = 2 * left.shape[0] * left.shape[1] * right.shape[1]
+        keep, send = run_kernel(weight_gradient, spot, (left, right), [shape, shape], [], flops)
+        return wide_sum(keep, swap(send, "x"), ring)
+
+    grad_fc2 = weight_grad(act, gy_rows, units)
+    grad_fc1 = weight_grad(h2_all, dpreb, 4 * shard)
+    dmid, dmidb, *dctx, sums2 = run_kernel(
+        middle_backward,
+        spot,
+        (*dh2, mid, gy_own, wo, named),
+        [((rows, width), F32), ((rows, width), BF16), *mine, ((8, width), F32)],
+        [],
+        2 * rows * width * width,
+    )
+    dctx = trade_rows(*dctx)
+    out_own, out_c = run_kernel(
+        out_rows_part,
+        spot,
+        (after(act, dh2[2]), wf2),
+        [pair_rows, pair_rows],
+        [],
+        2 * all_rows * width * wide,
+    )
+    out_terms = sum_rows(out_own, out_c)
+    ffn = out_terms[0][0].astype(F32) + out_terms[1][0].astype(F32) + out_terms[2].astype(F32)
+    result = (mid + ffn + row_of(named, BF2)).reshape(slots, count, width)
+    result = (live * result).astype(BF16)
+    half_ring = ((ring // 2, 4 * shard, 3 * part), BF16)
+    dh1_own, dh1_c, bq_sum, bv_sum, keep, send_far, send_near = run_kernel(
+        attention_backward,
+        spot,
+        (*dctx, q, k, v, probs, w_qkv, h1b),
+        [
+            pair_rows,
+            pair_rows,
+            ((1, part), F32),
+            ((1, part), F32),
+            ((ring, 4 * shard, 3 * part), BF16),
+            half_ring,
+            half_ring,
+        ],
+        [row_part, ((all_rows, 3 * part), BF16)],
+        2 * all_rows * part * (6 * width + 4 * frames),
+    )
+    far, near = swap(send_far, "x"), swap(send_near, "x")
+    half = ring // 2
+    others = [near[d] for d in range(half)] + [far[d] for d in range(half)]
+    grad_qkv = wide_sum(keep, others, ring)
+    dh1 = sum_rows(dh1_own, dh1_c)
+    grad_x, sums1 = run_kernel(
+        input_backward,
+        spot,
+        (*dh1, dmid, x_own, named),
+        [((rows, width), F32), ((8, width), F32)],
+        [],
+        rows * width,
+    )
+
+    quarters = ((2, ring, 2 * shard, width), BF16)
+    own, along_c = run_kernel(
+        out_gradient,
+        spot,
+        (*ctx, dmidb),
+        [quarters, quarters],
+        [((8, shard, width), F32)],
+        2 * rows * width * width,
+    )
+    over_c = swap(along_c, "c")
+    over_y = swap((own[1].astype(F32) + over_c[1].astype(F32)).astype(BF16), "y")
+    quarter = own[0].astype(F32) + over_c[0].astype(F32) + over_y.astype(F32)
+    grad_o = wide_sum(quarter[:, :shard], swap(quarter[:, shard:].astype(BF16), "x"), ring)
+
+    back = grad_fc1.astype(BF16).reshape(4, shard, groups, units)
+    grad_fc1 = trade_four(back).transpose(1, 2, 0, 3).reshape(shard, 4 * wide).astype(F32)
+    back = trade_four(grad_qkv.astype(BF16).reshape(4, shard, 3 * part)).astype(F32)
+    grad_q, grad_k, grad_v = [
+        back[:, :, n * part : (n + 1) * part].transpose(1, 0, 2).reshape(shard, width)
+        for n in range(3)
+    ]
+
+    mine = (jnp.arange(4) == me).astype(F32)[:, None]
+    spread = lambda value: mine * jnp.pad(value, ((0, 0), (0, width - value.shape[1])))
+    packed = jnp.concatenate(
+        [sums1[:2], sums2[:4], spread(dpre_sum), spread(bq_sum), spread(bv_sum), sums1[2:]]
+    )
+    for axis in ("c", "y", "x"):
+        packed = packed + swap(packed, axis)
+    packed = packed + sum(far_in_z(packed, d, ring) for d in range(1, ring))
+    at = (2 * z + x) * 4 + me
+    own = lax.dynamic_slice(packed, (0, at * shard), (6, shard))
+    grad_bf1 = lax.dynamic_slice(packed, (6 + me, (2 * z + x) * units), (1, units))[0]
+    per_part = part // shard
+    head_row, head_at = at // per_part, lax.rem(at, per_part) * shard
+    grad_bq = lax.dynamic_slice(packed, (10 + head_row, head_at), (1, shard))[0]
+    grad_bv = lax.dynamic_slice(packed, (14 + head_row, head_at), (1, shard))[0]
+    return (
+        result,
+        grad_x.reshape(slots, count, width),
+        own[0],
+        own[1],
+        grad_q,
+        grad_bq,
+        grad_k,
+        grad_v,
+        grad_bv,
+        grad_o,
+        own[2],
+        own[3],
+        own[4],
+        grad_fc1,
+        grad_bf1,
+        grad_fc2,
+        own[5],
+    )
+
+
 def solution(mesh):
+    clips, seqs = mesh.shape["clip"], mesh.shape["seq"]
+    ring = clips // 4
+    split = seqs == 2 and clips % 4 == 0 and ring & (ring - 1) == 0
+    if split:
+        names, both = ("z", "x", "c"), ("z", "x", "c", "y")
+        grid = Mesh(mesh.devices.reshape(ring, 2, 2, 2), both)
+        body, seq = functools.partial(on_device_split, ring), "y"
+    else:
+        names, both = ("clip",), ("clip", "seq")
+        grid, body, seq = mesh, on_device_gathered, "seq"
+    rows3 = P(names, seq, None)
+    vector, matrix = P(both), P(both, None)
     in_specs = (
-        P("clip", "seq", None),
-        P("clip"),
-        P(("clip", "seq")),
-        P(("clip", "seq")),
-        P(("clip", "seq"), None),
-        P(("clip", "seq")),
-        P(("clip", "seq"), None),
-        P(("clip", "seq"), None),
-        P(("clip", "seq")),
-        P(("clip", "seq"), None),
-        P(("clip", "seq")),
-        P(("clip", "seq")),
-        P(("clip", "seq")),
-        P(("clip", "seq"), None),
-        P(("clip", "seq")),
-        P(("clip", "seq"), None),
-        P(("clip", "seq")),
-        P("clip", "seq", None),
+        rows3, P(names), vector, vector, matrix, vector, matrix, matrix, vector, matrix,
+        vector, vector, vector, matrix, vector, matrix, vector, rows3,
     )
     out_specs = (
-        P("clip", "seq", None),
-        P("clip", "seq", None),
-        P(("clip", "seq")),
-        P(("clip", "seq")),
-        P(("clip", "seq"), None),
-        P(("clip", "seq")),
-        P(("clip", "seq"), None),
-        P(("clip", "seq"), None),
-        P(("clip", "seq")),
-        P(("clip", "seq"), None),
-        P(("clip", "seq")),
-        P(("clip", "seq")),
-        P(("clip", "seq")),
-        P(("clip", "seq"), None),
-        P(("clip", "seq")),
-        P(("clip", "seq"), None),
-        P(("clip", "seq")),
+        rows3, rows3, vector, vector, matrix, vector, matrix, matrix, vector, matrix,
+        vector, vector, vector, matrix, vector, matrix, vector,
     )
     return jax.shard_map(
-        on_device, mesh=mesh, in_specs=in_specs, out_specs=out_specs, check_vma=False
-    )
+        body, mesh=grid, in_specs=in_specs, out_specs=out_specs, check_vma=False
+    )

time: 802 us -> 291 us (0.36)
  waiting for transfers between devices: 575 us -> 121 us
  blocking collectives: 98.1 us -> 0 us
  matrix products: 68.8 us -> 0 us
  starting transfers between devices: 0.39 us -> 67.1 us
  Pallas kernels: 0 us -> 42.3 us
  local copies, waits for them, and re-layouts: 29.6 us -> 50.9 us
  between operations: 14.8 us -> 1.78 us
    reduce_scatter x4 -> x0, waiting for transfers between devices: 306 us -> none  [the longest x1 150 us: on_device(): lax.psum_scatter(jnp.concatenate([tdot(first_cols, dqb), tdot(first_cols,...]
    all_gather x6 -> x0, waiting for transfers between devices: 265 us -> none  [the longest x1 63.2 us: on_device(): lax.all_gather(w_fc1, ('clip', 'seq'), axis=0, tiled=True)]
    ppermute x0 -> x78, waiting for transfers between devices: none -> 121 us  [the longest x54 82.8 us: swap(): return lax.ppermute(value, axis, SWAP)]
    unnamed x2 -> x0, blocking collectives: 82.9 us -> none
    dot_general x24 -> x0, matrix products: 68.8 us -> none  [the longest x18 45.2 us: tdot(): return jnp.dot(left, right, preferred_element_type=jnp.float32)]
    ppermute x0 -> x78, starting transfers between devices: none -> 67.1 us  [the longest x54 35.2 us: swap(): return lax.ppermute(value, axis, SWAP)]
    pallas_call x0 -> x10, Pallas kernels: none -> 42.3 us  [run_kernel(): pl.pallas_call(body, in_specs=[pl.BlockSpec(memory_space=pltpu.SMEM)] + [...]
    dynamic_update_slice x0 -> x36, local copies, waits for them, and re-layouts: none -> 28.1 us  [the longest x33 25.1 us: wide_gather(): lax.dynamic_update_slice(outs[n], value[None, start:start + size], (at, 0...]
  transfers between devices with their start and end apart: 10 -> 78, of which waited for: 9 -> 40; matrix products, arithmetic and copies ran while one was open for 8% -> 18% of each run, Pallas kernels for 0% -> 11%
where the time goes in v2:
time: 291 us; the launch traced here: 290 us
  waiting for transfers between devices  121 us (42%)
  starting transfers between devices  67.1 us (23%)
  local copies, waits for them, and re-layouts  50.9 us (17%)
  Pallas kernels  42.3 us (15%)
  other arithmetic  6.77 us (2%)
    ppermute x54, waiting for transfers between devices, swap(): return lax.ppermute(value, axis, SWAP)  82.8 us
    pallas_call x10, Pallas kernels, run_kernel(): pl.pallas_call(body, in_specs=[pl.BlockSpec(memory_space=pltpu.SMEM)] + [...  42.3 us
    ppermute x24, waiting for transfers between devices, far_in_z(): lax.ppermute(value, 'z', tuple(((i, i ^ distance) for i in range(ring))))  38.2 us
    ppermute x54, starting transfers between devices, swap(): return lax.ppermute(value, axis, SWAP)  35.2 us
    ppermute x24, starting transfers between devices, far_in_z(): lax.ppermute(value, 'z', tuple(((i, i ^ distance) for i in range(ring))))  31.9 us
    dynamic_update_slice x33, local copies, waits for them, and re-layouts, wide_gather(): lax.dynamic_update_slice(outs[n], value[None, start:start + size], (at, 0...  25.1 us
  transfers between devices with their start and end apart: 78, of which 40 were waited for; matrix products, arithmetic and copies ran while one was open for 18% of the time, Pallas kernels for 11%

profile of v2, /device:TPU:0, one launch (start us, length us, event | category | flops | bytes accessed | tf_op | source)
XLA Modules:
  0.0 289.9 jit_solution(7336151915339914254)
XLA Ops:
  0.7 3.1 %collective-permute-start = (bf16[2,64,768]{2,1,0:T(8,128)(2,1)}, bf16[2,64,768]{2,1,0:T(8,128)(2,1)S(1)}, u32[]{:S(2)}, u32[]{:S(2)}) collective-permute-start(bf16[2,64,768]{2,1,0:T(8,128)(2,1)} %x0.1), channel_id=1, source_target_pairs={{0,1},{1,0},{2,3},{3,2},{4,5},{5,4},{6,7},{7,6},{8,9},{9,8},{10,11... | collective-permute-start | bytes 589832 | tf_op jit(solution)/shard_map/ppermute | solution.py:539
  7.8 2.0 collective-permute-start.31
  16.5 3.9 %collective-permute-start.11 = (bf16[112,576]{1,0:T(8,128)(2,1)}, bf16[112,576]{1,0:T(8,128)(2,1)S(1)}, u32[]{:S(2)}, u32[]{:S(2)}) collective-permute-start(bf16[112,576]{1,0:T(8,128)(2,1)} %pad_maximum_fusion.3), channel_id=1, source_target_pairs={{0,24},{8,16},{16,8},{24,0},{1,25},{9,17},{17,9},{25,1},{2,26},{10... | collective-permute-start | bytes 387080 | tf_op jit(solution)/shard_map/ppermute | solution.py:576
  25.7 4.9 %collective-permute-done.7 = bf16[112,576]{1,0:T(8,128)(2,1)S(1)} collective-permute-done((bf16[112,576]{1,0:T(8,128)(2,1)}, bf16[112,576]{1,0:T(8,128)(2,1)S(1)}, u32[]{:S(2)}, u32[]{:S(2)}) %collective-permute-start.7) | collective-permute-done | bytes 129056 | tf_op jit(solution)/shard_map/ppermute | solution.py:576
  33.2 2.4 collective-permute-start.17
  44.3 2.4 collective-permute-done.19
  47.2 3.4 %collective-permute-done.20 = bf16[24,768]{1,0:T(8,128)(2,1)S(1)} collective-permute-done((bf16[24,768]{1,0:T(8,128)(2,1)S(1)}, bf16[24,768]{1,0:T(8,128)(2,1)S(1)}, u32[]{:S(2)}, u32[]{:S(2)}) %collective-permute-start.20) | collective-permute-done | bytes 36896 | tf_op jit(solution)/shard_map/ppermute | solution.py:539
  52.1 4.5 %collective-permute-done.21 = bf16[24,768]{1,0:T(8,128)(2,1)S(1)} collective-permute-done((bf16[24,768]{1,0:T(8,128)(2,1)}, bf16[24,768]{1,0:T(8,128)(2,1)S(1)}, u32[]{:S(2)}, u32[]{:S(2)}) %collective-permute-start.21) | collective-permute-done | bytes 36896 | tf_op jit(solution)/shard_map/ppermute | solution.py:576
  57.1 4.8 %collective-permute-done.12 = bf16[112,576]{1,0:T(8,128)(2,1)S(1)} collective-permute-done((bf16[112,576]{1,0:T(8,128)(2,1)}, bf16[112,576]{1,0:T(8,128)(2,1)S(1)}, u32[]{:S(2)}, u32[]{:S(2)}) %collective-permute-start.12) | collective-permute-done | bytes 129056 | tf_op jit(solution)/shard_map/ppermute | solution.py:539
  63.1 5.3 %collective-permute-done.10 = bf16[112,576]{1,0:T(8,128)(2,1)S(1)} collective-permute-done((bf16[112,576]{1,0:T(8,128)(2,1)}, bf16[112,576]{1,0:T(8,128)(2,1)S(1)}, u32[]{:S(2)}, u32[]{:S(2)}) %collective-permute-start.10) | collective-permute-done | bytes 129056 | tf_op jit(solution)/shard_map/ppermute | solution.py:539
  69.6 4.1 %collective-permute-done.8 = bf16[112,576]{1,0:T(8,128)(2,1)S(1)} collective-permute-done((bf16[112,576]{1,0:T(8,128)(2,1)}, bf16[112,576]{1,0:T(8,128)(2,1)S(1)}, u32[]{:S(2)}, u32[]{:S(2)}) %collective-permute-start.8) | collective-permute-done | bytes 129056 | tf_op jit(solution)/shard_map/ppermute | solution.py:539
  75.1 1.9 dynamic_update_slice.139
  77.0 1.9 dynamic_update_slice.140
  78.9 1.9 dynamic_update_slice.141
  82.8 1.9 dynamic_update_slice.143
  96.0 5.7 %attention_forward.1 = (bf16[512,768]{1,0:T(8,128)(2,1)}, bf16[512,192]{1,0:T(8,128)(2,1)}, bf16[512,192]{1,0:T(8,128)(2,1)}, bf16[512,192]{1,0:T(8,128)(2,1)}, ...) custom-call(s32[5]{0:T(128)} %copy-done.29, ...), custom_call_target="tpu_custom_call" | custom-call | flops 503316480 | bytes 4055040 | tf_op jit(solution)/shard_map/attention_forward/pallas_call | solution.py:525
  102.3 6.1 %collective-permute-done.13 = bf16[2,128,192]{2,1,0:T(8,128)(2,1)S(1)} collective-permute-done((bf16[2,128,192]{2,1,0:T(8,128)(2,1)}, bf16[2,128,192]{2,1,0:T(8,128)(2,1)S(1)}, u32[]{:S(2)}, u32[]{:S(2)}) %collective-permute-start.13) | collective-permute-done | bytes 98336 | tf_op jit(solution)/shard_map/ppermute | solution.py:539
  111.1 6.0 %collective-permute-done.34 = bf16[192,768]{1,0:T(8,128)(2,1)S(1)} collective-permute-done((bf16[192,768]{1,0:T(8,128)(2,1)S(1)}, bf16[192,768]{1,0:T(8,128)(2,1)S(1)}, u32[]{:S(2)}, u32[]{:S(2)}) %collective-permute-start.34) | collective-permute-done | bytes 294944 | tf_op jit(solution)/shard_map/ppermute | solution.py:576
  117.1 2.1 collective-permute-start.38
  121.6 4.4 %collective-permute-done.35 = bf16[192,768]{1,0:T(8,128)(2,1)S(1)} collective-permute-done((bf16[192,768]{1,0:T(8,128)(2,1)S(1)}, bf16[192,768]{1,0:T(8,128)(2,1)S(1)}, u32[]{:S(2)}, u32[]{:S(2)}) %collective-permute-start.35) | collective-permute-done | bytes 294944 | tf_op jit(solution)/shard_map/ppermute | solution.py:539
  126.7 2.5 collective-permute-done.37
  132.2 2.6 out_projection.1
  135.4 6.2 %collective-permute-done.25.a1 = bf16[128,768]{1,0:T(8,128)(2,1)S(1)} collective-permute-done((bf16[128,768]{1,0:T(8,128)(2,1)}, bf16[128,768]{1,0:T(8,128)(2,1)S(1)}, u32[]{:S(2)}, u32[]{:S(2)}) %collective-permute-start.25) | collective-permute-done | bytes 196640 | tf_op jit(solution)/shard_map/ppermute | solution.py:539
  143.7 6.8 %feed_forward.1 = (bf16[512,768]{1,0:T(8,128)(2,1)}, bf16[512,768]{1,0:T(8,128)(2,1)}, bf16[512,768]{1,0:T(8,128)(2,1)}, bf16[512,768]{1,0:T(8,128)(2,1)}, bf16[...) custom-call(s32[5]{0:T(128)} %copy-done.29, bf16[128,768]{1,0:T(8,128)(2,1)} %get-tuple-element.72.a0, ...), custom_call_target="tpu_custom_call" | custom-call | flops 1811939328 | bytes 7891968 | tf_op jit(solution)/shard_map/feed_forward/pallas_call | solution.py:525
  150.7 3.3 %weight_gradient.3 = (bf16[4,96,768]{2,1,0:T(8,128)(2,1)}, bf16[4,96,768]{2,1,0:T(8,128)(2,1)}) custom-call(s32[5]{0:T(128)} %copy-done.29, bf16[512,768]{1,0:T(8,128)(2,1)} %get-tuple-element.78.act.left, bf16[512,768]{1,0:T(8,128)(2,1)} %get-tuple-element.108.right), custom_call_target="tpu_custom_call" | custom-call | flops 603979776 | bytes 2752512 | tf_op jit(solution)/shard_map/weight_gradient/pallas_call | solution.py:525
  155.5 3.2 %weight_gradient.2 = (bf16[4,96,768]{2,1,0:T(8,128)(2,1)}, bf16[4,96,768]{2,1,0:T(8,128)(2,1)}) custom-call(s32[5]{0:T(128)} %copy-done.29, bf16[512,768]{1,0:T(8,128)(2,1)} %get-tuple-element.104.left, bf16[512,768]{1,0:T(8,128)(2,1)} %get-tuple-element.105.right), custom_call_target="tpu_custom_call" | custom-call | flops 603979776 | bytes 2752512 | tf_op jit(solution)/shard_map/weight_gradient/pallas_call | solution.py:525
  160.0 6.0 %collective-permute-done.41.d2 = bf16[128,768]{1,0:T(8,128)(2,1)S(1)} collective-permute-done((bf16[128,768]{1,0:T(8,128)(2,1)S(1)}, bf16[128,768]{1,0:T(8,128)(2,1)S(1)}, u32[]{:S(2)}, u32[]{:S(2)}) %collective-permute-start.41) | collective-permute-done | bytes 196640 | tf_op jit(solution)/shard_map/ppermute | solution.py:539
  166.7 3.2 %middle_backward.1 = (f32[128,768]{1,0:T(8,128)}, bf16[128,768]{1,0:T(8,128)(2,1)}, bf16[128,192]{1,0:T(8,128)(2,1)}, bf16[2,128,192]{2,1,0:T(8,128)(2,1)}, bf16[128,192]{1,0:T(8,128)(2,1)}, /*index=5*/f32[8,768]{1,0:T(8,128)}) custom-call(s32[5]{0:T(128)} %copy-done.29, bf16[2,128,768]{2,1,0:T(8,128)(2,1)} %get-tuple-element.76.d0, ...), custom_call_target="tpu_custom_call" | custom-call | flops 150994944 | bytes 3588096 | tf_op jit(solution)/shard_map/middle_backward/pallas_call | solution.py:525
  171.2 3.1 %out_rows_part.1 = (bf16[2,128,768]{2,1,0:T(8,128)(2,1)}, bf16[2,128,768]{2,1,0:T(8,128)(2,1)}) custom-call(s32[5]{0:T(128)} %copy-done.29, bf16[512,768]{1,0:T(8,128)(2,1)} %get-tuple-element.78.act.left, bf16[768,768]{1,0:T(8,128)(2,1)} %bitcast.306), custom_call_target="tpu_custom_call" | custom-call | flops 603979776 | bytes 2752512 | tf_op jit(solution)/shard_map/out_rows_part/pallas_call | solution.py:525
  174.7 7.8 %collective-permute-done.68 = bf16[4,96,768]{2,1,0:T(8,128)(2,1)S(1)} collective-permute-done((bf16[4,96,768]{2,1,0:T(8,128)(2,1)}, bf16[4,96,768]{2,1,0:T(8,128)(2,1)S(1)}, u32[]{:S(2)}, u32[]{:S(2)}) %collective-permute-start.68) | collective-permute-done | bytes 589856 | tf_op jit(solution)/shard_map/ppermute | solution.py:539
  184.3 2.7 out_gradient.1
  187.0 2.7 collective-permute-start.70
  192.8 2.1 collective-permute-done.71
  195.0 5.9 %collective-permute-done.70 = bf16[96,768]{1,0:T(8,128)(2,1)S(1)} collective-permute-done((bf16[96,768]{1,0:T(8,128)(2,1)S(1)}, bf16[96,768]{1,0:T(8,128)(2,1)S(1)}, u32[]{:S(2)}, u32[]{:S(2)}) %collective-permute-start.70) | collective-permute-done | bytes 147488 | tf_op jit(solution)/shard_map/ppermute | solution.py:576
  202.8 9.1 %attention_backward.1 = (bf16[2,128,768]{2,1,0:T(8,128)(2,1)}, bf16[2,128,768]{2,1,0:T(8,128)(2,1)}, f32[1,192]{1,0:T(1,128)}, f32[1,192]{1,0:T(1,128)}, bf16[4,...) custom-call(s32[5]{0:T(128)} %copy-done.29, ...), custom_call_target="tpu_custom_call" | custom-call | flops 1006632960 | bytes 4916736 | tf_op jit(solution)/shard_map/attention_backward/pallas_call | solution.py:525
  216.6 2.3 collective-permute-done.72
  221.3 4.5 %collective-permute-done.56 = bf16[2,96,576]{2,1,0:T(8,128)(2,1)S(1)} collective-permute-done((bf16[2,96,576]{2,1,0:T(8,128)(2,1)}, bf16[2,96,576]{2,1,0:T(8,128)(2,1)S(1)}, u32[]{:S(2)}, u32[]{:S(2)}) %collective-permute-start.56) | collective-permute-done | bytes 221216 | tf_op jit(solution)/shard_map/ppermute | solution.py:539
  225.9 2.0 collective-permute-start.57
  231.7 2.2 collective-permute-done.57
  234.0 5.5 %collective-permute-done.58 = bf16[96,576]{1,0:T(8,128)(2,1)S(1)} collective-permute-done((bf16[96,576]{1,0:T(8,128)(2,1)S(1)}, bf16[96,576]{1,0:T(8,128)(2,1)S(1)}, u32[]{:S(2)}, u32[]{:S(2)}) %collective-permute-start.58) | collective-permute-done | bytes 110624 | tf_op jit(solution)/shard_map/ppermute | solution.py:576
  241.8 2.7 collective-permute-done.60
  248.0 4.1 %collective-permute-done.48.d2 = bf16[128,768]{1,0:T(8,128)(2,1)S(1)} collective-permute-done((bf16[128,768]{1,0:T(8,128)(2,1)S(1)}, bf16[128,768]{1,0:T(8,128)(2,1)S(1)}, u32[]{:S(2)}, u32[]{:S(2)}) %collective-permute-start.48) | collective-permute-done | bytes 196640 | tf_op jit(solution)/shard_map/ppermute | solution.py:539
  252.8 2.5 input_backward.1
  259.4 8.8 %collective-permute-done.50 = f32[24,768]{1,0:T(8,128)S(1)} collective-permute-done((f32[24,768]{1,0:T(8,128)S(1)}, f32[24,768]{1,0:T(8,128)S(1)}, u32[]{:S(2)}, u32[]{:S(2)}) %collective-permute-start.50) | collective-permute-done | bytes 73760 | tf_op jit(solution)/shard_map/ppermute | solution.py:539
  272.6 1.9 collective-permute-start.54
  274.6 2.5 collective-permute-start.52
  282.4 1.9 collective-permute-start.65
  284.4 2.5 collective-permute-start.66
  (351 shorter events, 104.5 us)
Async XLA Ops:
  0.7 23.2 %collective-permute-start = (bf16[2,64,768]{2,1,0:T(8,128)(2,1)}, bf16[2,64,768]{2,1,0:T(8,128)(2,1)S(1)}, u32[]{:S(2)}, u32[]{:S(2)}) collective-permute-start(bf16[2,64,768]{2,1,0:T(8,128)(2,1)} %x0.1), channel_id=1, source_target_pairs={{0,1},{1,0},{2,3},{3,2},{4,5},{5,4},{6,7},{7,6},{8,9},{9,8},{10,11... | collective-permute-start | bytes 589832 | tf_op jit(solution)/shard_map/ppermute | solution.py:539
  3.7 90.2 %collective-permute-start.1 = (bf16[2,64,768]{2,1,0:T(8,128)(2,1)}, bf16[2,64,768]{2,1,0:T(8,128)(2,1)}, u32[]{:S(2)}, u32[]{:S(2)}) collective-permute-start(bf16[2,64,768]{2,1,0:T(8,128)(2,1)} %x0.1), channel_id=1, source_target_pairs={{0,2},{2,0},{1,3},{3,1},{4,6},{6,4},{5,7},{7,5},{8,10},{10,8},{9,1... | collective-permute-start | bytes 589832 | tf_op jit(solution)/shard_map/ppermute | solution.py:539
  12.5 10.7 %collective-permute-start.32 = (bf16[2,24,768]{2,1,0:T(8,128)(2,1)S(1)}, bf16[2,24,768]{2,1,0:T(8,128)(2,1)S(1)}, u32[]{:S(2)}, u32[]{:S(2)}) collective-permute-start(bf16[2,24,768]{2,1,0:T(8,128)(2,1)S(1)} %get-tuple-element.153), channel_id=1, source_target_pairs={{0,2},{2,0},{1,3},{3,1},{4,6},{6,4},{5,7},{7,5},{8,10},{10,8},{9,1... | collective-permute-start | bytes 221192 | tf_op jit(solution)/shard_map/ppermute | solution.py:539
  16.5 14.0 %collective-permute-start.11 = (bf16[112,576]{1,0:T(8,128)(2,1)}, bf16[112,576]{1,0:T(8,128)(2,1)S(1)}, u32[]{:S(2)}, u32[]{:S(2)}) collective-permute-start(bf16[112,576]{1,0:T(8,128)(2,1)} %pad_maximum_fusion.3), channel_id=1, source_target_pairs={{0,24},{8,16},{16,8},{24,0},{1,25},{9,17},{17,9},{25,1},{2,26},{10... | collective-permute-start | bytes 387080 | tf_op jit(solution)/shard_map/ppermute | solution.py:576
  20.4 16.6 %collective-permute-start.9 = (bf16[112,576]{1,0:T(8,128)(2,1)}, bf16[112,576]{1,0:T(8,128)(2,1)}, u32[]{:S(2)}, u32[]{:S(2)}) collective-permute-start(bf16[112,576]{1,0:T(8,128)(2,1)} %pad_maximum_fusion.3), channel_id=1, source_target_pairs={{0,16},{8,24},{16,0},{24,8},{1,17},{9,25},{17,1},{25,9},{2,18},{10... | collective-permute-start | bytes 387080 | tf_op jit(solution)/shard_map/ppermute | solution.py:576
  23.2 7.3 %collective-permute-start.7 = (bf16[112,576]{1,0:T(8,128)(2,1)}, bf16[112,576]{1,0:T(8,128)(2,1)S(1)}, u32[]{:S(2)}, u32[]{:S(2)}) collective-permute-start(bf16[112,576]{1,0:T(8,128)(2,1)} %pad_maximum_fusion.3), channel_id=1, source_target_pairs={{0,8},{8,0},{16,24},{24,16},{1,9},{9,1},{17,25},{25,17},{2,10},{10... | collective-permute-start | bytes 387080 | tf_op jit(solution)/shard_map/ppermute | solution.py:576
  23.9 9.3 %collective-permute-start.6 = (bf16[112,576]{1,0:T(8,128)(2,1)}, bf16[112,576]{1,0:T(8,128)(2,1)S(1)}, u32[]{:S(2)}, u32[]{:S(2)}) collective-permute-start(bf16[112,576]{1,0:T(8,128)(2,1)} %pad_maximum_fusion.3), channel_id=1, source_target_pairs={{0,4},{4,0},{1,5},{5,1},{2,6},{6,2},{3,7},{7,3},{8,12},{12,8},{9,1... | collective-permute-start | bytes 387080 | tf_op jit(solution)/shard_map/ppermute | solution.py:539
  30.5 111.1 %collective-permute-start.29 = (bf16[128,768]{1,0:T(8,128)(2,1)S(1)}, bf16[128,768]{1,0:T(8,128)(2,1)}, u32[]{:S(2)}, u32[]{:S(2)}) collective-permute-start(bf16[128,768]{1,0:T(8,128)(2,1)S(1)} %bitcast.312), channel_id=1, source_target_pairs={{0,2},{2,0},{1,3},{3,1},{4,6},{6,4},{5,7},{7,5},{8,10},{10,8},{9,1... | collective-permute-start | bytes 589832 | tf_op jit(solution)/shard_map/ppermute | solution.py:539
  30.6 95.6 %collective-permute-start.28 = (bf16[128,768]{1,0:T(8,128)(2,1)S(1)}, bf16[128,768]{1,0:T(8,128)(2,1)}, u32[]{:S(2)}, u32[]{:S(2)}) collective-permute-start(bf16[128,768]{1,0:T(8,128)(2,1)S(1)} %bitcast.313), channel_id=1, source_target_pairs={{0,1},{1,0},{2,3},{3,2},{4,5},{5,4},{6,7},{7,6},{8,9},{9,8},{10,11... | collective-permute-start | bytes 589832 | tf_op jit(solution)/shard_map/ppermute | solution.py:539
  33.2 8.3 %collective-permute-start.17 = (bf16[24,768]{1,0:T(8,128)(2,1)}, bf16[24,768]{1,0:T(8,128)(2,1)}, u32[]{:S(2)}, u32[]{:S(2)}) collective-permute-start(bf16[24,768]{1,0:T(8,128)(2,1)} %param.27), channel_id=1, source_target_pairs={{0,8},{8,0},{16,24},{24,16},{1,9},{9,1},{17,25},{25,17},{2,10},{10... | collective-permute-start | bytes 110600 | tf_op jit(solution)/shard_map/ppermute | solution.py:576
  46.7 48.1 %collective-permute-start.2 = (bf16[2,64,768]{2,1,0:T(8,128)(2,1)}, bf16[2,64,768]{2,1,0:T(8,128)(2,1)}, u32[]{:S(2)}, u32[]{:S(2)}) collective-permute-start(bf16[2,64,768]{2,1,0:T(8,128)(2,1)} %copy-done.36), channel_id=1, source_target_pairs={{0,2},{2,0},{1,3},{3,1},{4,6},{6,4},{5,7},{7,5},{8,10},{10,8},{9,1... | collective-permute-start | bytes 589832 | tf_op jit(solution)/shard_map/ppermute | solution.py:539
  73.8 45.5 %collective-permute-start.36 = (bf16[192,768]{1,0:T(8,128)(2,1)S(1)}, bf16[192,768]{1,0:T(8,128)(2,1)S(1)}, u32[]{:S(2)}, u32[]{:S(2)}) collective-permute-start(bf16[192,768]{1,0:T(8,128)(2,1)S(1)} %pad_maximum_fusion.2), channel_id=1, source_target_pairs={{0,16},{8,24},{16,0},{24,8},{1,17},{9,25},{17,1},{25,9},{2,18},{10... | collective-permute-start | bytes 884744 | tf_op jit(solution)/shard_map/ppermute | solution.py:576
  93.9 16.7 %collective-permute-start.33 = (bf16[192,768]{1,0:T(8,128)(2,1)S(1)}, bf16[192,768]{1,0:T(8,128)(2,1)S(1)}, u32[]{:S(2)}, u32[]{:S(2)}) collective-permute-start(bf16[192,768]{1,0:T(8,128)(2,1)S(1)} %pad_maximum_fusion.2), channel_id=1, source_target_pairs={{0,4},{4,0},{1,5},{5,1},{2,6},{6,2},{3,7},{7,3},{8,12},{12,8},{9,1... | collective-permute-start | bytes 884744 | tf_op jit(solution)/shard_map/ppermute | solution.py:539
  94.8 7.0 %collective-permute-start.22 = (bf16[24,768]{1,0:T(8,128)(2,1)S(1)}, bf16[24,768]{1,0:T(8,128)(2,1)S(1)}, u32[]{:S(2)}, u32[]{:S(2)}) collective-permute-start(bf16[24,768]{1,0:T(8,128)(2,1)S(1)} %copy-done.28), channel_id=1, source_target_pairs={{0,4},{4,0},{1,5},{5,1},{2,6},{6,2},{3,7},{7,3},{8,12},{12,8},{9,1... | collective-permute-start | bytes 110600 | tf_op jit(solution)/shard_map/ppermute | solution.py:539
  101.7 6.6 %collective-permute-start.13 = (bf16[2,128,192]{2,1,0:T(8,128)(2,1)}, bf16[2,128,192]{2,1,0:T(8,128)(2,1)S(1)}, u32[]{:S(2)}, u32[]{:S(2)}) collective-permute-start(bf16[2,128,192]{2,1,0:T(8,128)(2,1)} %get-tuple-element.68), channel_id=1, source_target_pairs={{0,1},{1,0},{2,3},{3,2},{4,5},{5,4},{6,7},{7,6},{8,9},{9,8},{10,11... | collective-permute-start | bytes 294920 | tf_op jit(solution)/shard_map/ppermute | solution.py:539
  108.4 8.7 %collective-permute-start.34 = (bf16[192,768]{1,0:T(8,128)(2,1)S(1)}, bf16[192,768]{1,0:T(8,128)(2,1)S(1)}, u32[]{:S(2)}, u32[]{:S(2)}) collective-permute-start(bf16[192,768]{1,0:T(8,128)(2,1)S(1)} %pad_maximum_fusion.2), channel_id=1, source_target_pairs={{0,8},{8,0},{16,24},{24,16},{1,9},{9,1},{17,25},{25,17},{2,10},{10... | collective-permute-start | bytes 884744 | tf_op jit(solution)/shard_map/ppermute | solution.py:576
  110.6 9.3 %collective-permute-start.23 = (bf16[8,24,768]{2,1,0:T(8,128)(2,1)S(1)}, bf16[8,24,768]{2,1,0:T(8,128)(2,1)S(1)}, u32[]{:S(2)}, u32[]{:S(2)}) collective-permute-start(bf16[8,24,768]{2,1,0:T(8,128)(2,1)S(1)} %bitcast_dynamic-update-slice_fusion.4), channel_id=1, source_target_pairs={{0,1},{1,0},{2,3},{3,2},{4,5},{5,4},{6,7},{7,6},{8,9},{9,8},{10,11... | collective-permute-start | bytes 884744 | tf_op jit(solution)/shard_map/ppermute | solution.py:539
  117.1 12.1 %collective-permute-start.38 = (bf16[192,768]{1,0:T(8,128)(2,1)S(1)}, bf16[192,768]{1,0:T(8,128)(2,1)S(1)}, u32[]{:S(2)}, u32[]{:S(2)}) collective-permute-start(bf16[192,768]{1,0:T(8,128)(2,1)S(1)} %pad_maximum_fusion.2), channel_id=1, source_target_pairs={{0,24},{8,16},{16,8},{24,0},{1,25},{9,17},{17,9},{25,1},{2,26},{10... | collective-permute-start | bytes 884744 | tf_op jit(solution)/shard_map/ppermute | solution.py:576
  119.3 6.8 %collective-permute-start.35 = (bf16[192,768]{1,0:T(8,128)(2,1)S(1)}, bf16[192,768]{1,0:T(8,128)(2,1)S(1)}, u32[]{:S(2)}, u32[]{:S(2)}) collective-permute-start(bf16[192,768]{1,0:T(8,128)(2,1)S(1)} %collective-permute-done.34), channel_id=1, source_target_pairs={{0,4},{4,0},{1,5},{5,1},{2,6},{6,2},{3,7},{7,3},{8,12},{12,8},{9,1... | collective-permute-start | bytes 884744 | tf_op jit(solution)/shard_map/ppermute | solution.py:539
  119.9 9.3 %collective-permute-start.37 = (bf16[192,768]{1,0:T(8,128)(2,1)S(1)}, bf16[192,768]{1,0:T(8,128)(2,1)S(1)}, u32[]{:S(2)}, u32[]{:S(2)}) collective-permute-start(bf16[192,768]{1,0:T(8,128)(2,1)S(1)} %collective-permute-done.36), channel_id=1, source_target_pairs={{0,4},{4,0},{1,5},{5,1},{2,6},{6,2},{3,7},{7,3},{8,12},{12,8},{9,1... | collective-permute-start | bytes 884744 | tf_op jit(solution)/shard_map/ppermute | solution.py:539
  129.2 12.5 %collective-permute-start.30 = (bf16[128,768]{1,0:T(8,128)(2,1)}, bf16[128,768]{1,0:T(8,128)(2,1)S(1)}, u32[]{:S(2)}, u32[]{:S(2)}) collective-permute-start(bf16[128,768]{1,0:T(8,128)(2,1)} %collective-permute-done.28.g1), channel_id=1, source_target_pairs={{0,2},{2,0},{1,3},{3,1},{4,6},{6,4},{5,7},{7,5},{8,10},{10,8},{9,1... | collective-permute-start | bytes 589832 | tf_op jit(solution)/shard_map/ppermute | solution.py:539
  129.8 11.8 %collective-permute-start.39 = (bf16[192,768]{1,0:T(8,128)(2,1)S(1)}, bf16[192,768]{1,0:T(8,128)(2,1)S(1)}, u32[]{:S(2)}, u32[]{:S(2)}) collective-permute-start(bf16[192,768]{1,0:T(8,128)(2,1)S(1)} %collective-permute-done.38), channel_id=1, source_target_pairs={{0,4},{4,0},{1,5},{5,1},{2,6},{6,2},{3,7},{7,3},{8,12},{12,8},{9,1... | collective-permute-start | bytes 884744 | tf_op jit(solution)/shard_map/ppermute | solution.py:539
  134.8 6.8 %collective-permute-start.25 = (bf16[128,768]{1,0:T(8,128)(2,1)}, bf16[128,768]{1,0:T(8,128)(2,1)S(1)}, u32[]{:S(2)}, u32[]{:S(2)}) collective-permute-start(bf16[128,768]{1,0:T(8,128)(2,1)} %get-tuple-element.72.a0), channel_id=1, source_target_pairs={{0,1},{1,0},{2,3},{3,2},{4,5},{5,4},{6,7},{7,6},{8,9},{9,8},{10,11... | collective-permute-start | bytes 589832 | tf_op jit(solution)/shard_map/ppermute | solution.py:539
  150.6 8.7 %collective-permute-start.40 = (bf16[2,128,768]{2,1,0:T(8,128)(2,1)}, bf16[2,128,768]{2,1,0:T(8,128)(2,1)S(1)}, u32[]{:S(2)}, u32[]{:S(2)}) collective-permute-start(bf16[2,128,768]{2,1,0:T(8,128)(2,1)} %get-tuple-element.77), channel_id=1, source_target_pairs={{0,2},{2,0},{1,3},{3,1},{4,6},{6,4},{5,7},{7,5},{8,10},{10,8},{9,1... | collective-permute-start | bytes 1179656 | tf_op jit(solution)/shard_map/ppermute | solution.py:539
  154.0 20.6 %collective-permute-start.74 = (bf16[4,96,768]{2,1,0:T(8,128)(2,1)}, bf16[4,96,768]{2,1,0:T(8,128)(2,1)S(1)}, u32[]{:S(2)}, u32[]{:S(2)}) collective-permute-start(bf16[4,96,768]{2,1,0:T(8,128)(2,1)} %get-tuple-element.110), channel_id=1, source_target_pairs={{0,4},{4,0},{1,5},{5,1},{2,6},{6,2},{3,7},{7,3},{8,12},{12,8},{9,1... | collective-permute-start | bytes 1769480 | tf_op jit(solution)/shard_map/ppermute | solution.py:539
  158.7 23.7 %collective-permute-start.68 = (bf16[4,96,768]{2,1,0:T(8,128)(2,1)}, bf16[4,96,768]{2,1,0:T(8,128)(2,1)S(1)}, u32[]{:S(2)}, u32[]{:S(2)}) collective-permute-start(bf16[4,96,768]{2,1,0:T(8,128)(2,1)} %get-tuple-element.107), channel_id=1, source_target_pairs={{0,4},{4,0},{1,5},{5,1},{2,6},{6,2},{3,7},{7,3},{8,12},{12,8},{9,1... | collective-permute-start | bytes 1769480 | tf_op jit(solution)/shard_map/ppermute | solution.py:539
  159.3 6.7 %collective-permute-start.41 = (bf16[128,768]{1,0:T(8,128)(2,1)S(1)}, bf16[128,768]{1,0:T(8,128)(2,1)S(1)}, u32[]{:S(2)}, u32[]{:S(2)}) collective-permute-start(bf16[128,768]{1,0:T(8,128)(2,1)S(1)} %fusion.11), channel_id=1, source_target_pairs={{0,1},{1,0},{2,3},{3,2},{4,5},{5,4},{6,7},{7,6},{8,9},{9,8},{10,11... | collective-permute-start | bytes 589832 | tf_op jit(solution)/shard_map/ppermute | solution.py:539
  170.7 30.3 %collective-permute-start.45 = (bf16[128,192]{1,0:T(8,128)(2,1)}, bf16[128,192]{1,0:T(8,128)(2,1)S(1)}, u32[]{:S(2)}, u32[]{:S(2)}) collective-permute-start(bf16[128,192]{1,0:T(8,128)(2,1)} %get-tuple-element.83), channel_id=1, source_target_pairs={{0,2},{2,0},{1,3},{3,1},{4,6},{6,4},{5,7},{7,5},{8,10},{10,8},{9,1... | collective-permute-start | bytes 147464 | tf_op jit(solution)/shard_map/ppermute | solution.py:539
  170.7 16.3 %collective-permute-start.44 = (bf16[2,128,192]{2,1,0:T(8,128)(2,1)}, bf16[2,128,192]{2,1,0:T(8,128)(2,1)S(1)}, u32[]{:S(2)}, u32[]{:S(2)}) collective-permute-start(bf16[2,128,192]{2,1,0:T(8,128)(2,1)} %get-tuple-element.82), channel_id=1, source_target_pairs={{0,1},{1,0},{2,3},{3,2},{4,5},{5,4},{6,7},{7,6},{8,9},{9,8},{10,11... | collective-permute-start | bytes 294920 | tf_op jit(solution)/shard_map/ppermute | solution.py:539
  174.3 65.8 %collective-permute-start.42 = (bf16[2,128,768]{2,1,0:T(8,128)(2,1)}, bf16[2,128,768]{2,1,0:T(8,128)(2,1)S(1)}, u32[]{:S(2)}, u32[]{:S(2)}) collective-permute-start(bf16[2,128,768]{2,1,0:T(8,128)(2,1)} %get-tuple-element.80), channel_id=1, source_target_pairs={{0,2},{2,0},{1,3},{3,1},{4,6},{6,4},{5,7},{7,5},{8,10},{10,8},{9,1... | collective-permute-start | bytes 1179656 | tf_op jit(solution)/shard_map/ppermute | solution.py:539
  182.5 8.6 %collective-permute-start.69 = (bf16[96,768]{1,0:T(8,128)(2,1)S(1)}, bf16[96,768]{1,0:T(8,128)(2,1)S(1)}, u32[]{:S(2)}, u32[]{:S(2)}) collective-permute-start(bf16[96,768]{1,0:T(8,128)(2,1)S(1)} %get-tuple-element.120), channel_id=1, source_target_pairs={{0,24},{8,16},{16,8},{24,0},{1,25},{9,17},{17,9},{25,1},{2,26},{10... | collective-permute-start | bytes 442376 | tf_op jit(solution)/shard_map/ppermute | solution.py:576
  184.3 10.6 %collective-permute-start.71 = (bf16[96,768]{1,0:T(8,128)(2,1)S(1)}, bf16[96,768]{1,0:T(8,128)(2,1)S(1)}, u32[]{:S(2)}, u32[]{:S(2)}) collective-permute-start(bf16[96,768]{1,0:T(8,128)(2,1)S(1)} %get-tuple-element.121), channel_id=1, source_target_pairs={{0,8},{8,0},{16,24},{24,16},{1,9},{9,1},{17,25},{25,17},{2,10},{10... | collective-permute-start | bytes 442376 | tf_op jit(solution)/shard_map/ppermute | solution.py:576
  187.0 13.9 %collective-permute-start.70 = (bf16[96,768]{1,0:T(8,128)(2,1)S(1)}, bf16[96,768]{1,0:T(8,128)(2,1)S(1)}, u32[]{:S(2)}, u32[]{:S(2)}) collective-permute-start(bf16[96,768]{1,0:T(8,128)(2,1)S(1)} %get-tuple-element.122), channel_id=1, source_target_pairs={{0,16},{8,24},{16,0},{24,8},{1,17},{9,25},{17,1},{25,9},{2,18},{10... | collective-permute-start | bytes 442376 | tf_op jit(solution)/shard_map/ppermute | solution.py:576
  191.1 21.1 %collective-permute-start.75 = (bf16[96,768]{1,0:T(8,128)(2,1)S(1)}, bf16[96,768]{1,0:T(8,128)(2,1)S(1)}, u32[]{:S(2)}, u32[]{:S(2)}) collective-permute-start(bf16[96,768]{1,0:T(8,128)(2,1)S(1)} %get-tuple-element.117), channel_id=1, source_target_pairs={{0,24},{8,16},{16,8},{24,0},{1,25},{9,17},{17,9},{25,1},{2,26},{10... | collective-permute-start | bytes 442376 | tf_op jit(solution)/shard_map/ppermute | solution.py:576
  195.0 18.8 %collective-permute-start.77 = (bf16[96,768]{1,0:T(8,128)(2,1)S(1)}, bf16[96,768]{1,0:T(8,128)(2,1)}, u32[]{:S(2)}, u32[]{:S(2)}) collective-permute-start(bf16[96,768]{1,0:T(8,128)(2,1)S(1)} %get-tuple-element.118), channel_id=1, source_target_pairs={{0,8},{8,0},{16,24},{24,16},{1,9},{9,1},{17,25},{25,17},{2,10},{10... | collective-permute-start | bytes 442376 | tf_op jit(solution)/shard_map/ppermute | solution.py:576
  201.0 13.3 %collective-permute-start.76 = (bf16[96,768]{1,0:T(8,128)(2,1)S(1)}, bf16[96,768]{1,0:T(8,128)(2,1)}, u32[]{:S(2)}, u32[]{:S(2)}) collective-permute-start(bf16[96,768]{1,0:T(8,128)(2,1)S(1)} %get-tuple-element.119), channel_id=1, source_target_pairs={{0,16},{8,24},{16,0},{24,8},{1,17},{9,25},{17,1},{25,9},{2,18},{10... | collective-permute-start | bytes 442376 | tf_op jit(solution)/shard_map/ppermute | solution.py:576
  202.1 45.0 %collective-permute-start.62 = (bf16[2,4,48,768]{3,2,1,0:T(8,128)(2,1)}, bf16[2,4,48,768]{3,2,1,0:T(8,128)(2,1)S(1)}, u32[]{:S(2)}, u32[]{:S(2)}) collective-permute-start(bf16[2,4,48,768]{3,2,1,0:T(8,128)(2,1)} %get-tuple-element.103), channel_id=1, source_target_pairs={{0,2},{2,0},{1,3},{3,1},{4,6},{6,4},{5,7},{7,5},{8,10},{10,8},{9,1... | collective-permute-start | bytes 1769480 | tf_op jit(solution)/shard_map/ppermute | solution.py:539
  212.2 9.1 %collective-permute-start.55 = (bf16[2,96,576]{2,1,0:T(8,128)(2,1)}, bf16[2,96,576]{2,1,0:T(8,128)(2,1)S(1)}, u32[]{:S(2)}, u32[]{:S(2)}) collective-permute-start(bf16[2,96,576]{2,1,0:T(8,128)(2,1)} %get-tuple-element.99), channel_id=1, source_target_pairs={{0,4},{4,0},{1,5},{5,1},{2,6},{6,2},{3,7},{7,3},{8,12},{12,8},{9,1... | collective-permute-start | bytes 663560 | tf_op jit(solution)/shard_map/ppermute | solution.py:539
  213.8 12.0 %collective-permute-start.56 = (bf16[2,96,576]{2,1,0:T(8,128)(2,1)}, bf16[2,96,576]{2,1,0:T(8,128)(2,1)S(1)}, u32[]{:S(2)}, u32[]{:S(2)}) collective-permute-start(bf16[2,96,576]{2,1,0:T(8,128)(2,1)} %get-tuple-element.100), channel_id=1, source_target_pairs={{0,4},{4,0},{1,5},{5,1},{2,6},{6,2},{3,7},{7,3},{8,12},{12,8},{9,1... | collective-permute-start | bytes 663560 | tf_op jit(solution)/shard_map/ppermute | solution.py:539
  225.9 8.1 %collective-permute-start.57 = (bf16[96,576]{1,0:T(8,128)(2,1)S(1)}, bf16[96,576]{1,0:T(8,128)(2,1)S(1)}, u32[]{:S(2)}, u32[]{:S(2)}) collective-permute-start(bf16[96,576]{1,0:T(8,128)(2,1)S(1)} %get-tuple-element.126), channel_id=1, source_target_pairs={{0,24},{8,16},{16,8},{24,0},{1,25},{9,17},{17,9},{25,1},{2,26},{10... | collective-permute-start | bytes 331784 | tf_op jit(solution)/shard_map/ppermute | solution.py:576
  227.9 11.5 %collective-permute-start.58 = (bf16[96,576]{1,0:T(8,128)(2,1)S(1)}, bf16[96,576]{1,0:T(8,128)(2,1)S(1)}, u32[]{:S(2)}, u32[]{:S(2)}) collective-permute-start(bf16[96,576]{1,0:T(8,128)(2,1)S(1)} %get-tuple-element.127), channel_id=1, source_target_pairs={{0,16},{8,24},{16,0},{24,8},{1,17},{9,25},{17,1},{25,9},{2,18},{10... | collective-permute-start | bytes 331784 | tf_op jit(solution)/shard_map/ppermute | solution.py:576
  229.0 10.5 %collective-permute-start.59 = (bf16[96,576]{1,0:T(8,128)(2,1)S(1)}, bf16[96,576]{1,0:T(8,128)(2,1)S(1)}, u32[]{:S(2)}, u32[]{:S(2)}) collective-permute-start(bf16[96,576]{1,0:T(8,128)(2,1)S(1)} %get-tuple-element.130), channel_id=1, source_target_pairs={{0,8},{8,0},{16,24},{24,16},{1,9},{9,1},{17,25},{25,17},{2,10},{10... | collective-permute-start | bytes 331784 | tf_op jit(solution)/shard_map/ppermute | solution.py:576
  234.0 10.7 %collective-permute-start.47 = (bf16[2,128,768]{2,1,0:T(8,128)(2,1)}, bf16[2,128,768]{2,1,0:T(8,128)(2,1)S(1)}, u32[]{:S(2)}, u32[]{:S(2)}) collective-permute-start(bf16[2,128,768]{2,1,0:T(8,128)(2,1)} %get-tuple-element.90), channel_id=1, source_target_pairs={{0,2},{2,0},{1,3},{3,1},{4,6},{6,4},{5,7},{7,5},{8,10},{10,8},{9,1... | collective-permute-start | bytes 1179656 | tf_op jit(solution)/shard_map/ppermute | solution.py:539
  240.2 6.8 %collective-permute-start.43 = (bf16[128,768]{1,0:T(8,128)(2,1)S(1)}, bf16[128,768]{1,0:T(8,128)(2,1)S(1)}, u32[]{:S(2)}, u32[]{:S(2)}) collective-permute-start(bf16[128,768]{1,0:T(8,128)(2,1)S(1)} %fusion.12), channel_id=1, source_target_pairs={{0,1},{1,0},{2,3},{3,2},{4,5},{5,4},{6,7},{7,6},{8,9},{9,8},{10,11... | collective-permute-start | bytes 589832 | tf_op jit(solution)/shard_map/ppermute | solution.py:539
  244.7 7.3 %collective-permute-start.48 = (bf16[128,768]{1,0:T(8,128)(2,1)S(1)}, bf16[128,768]{1,0:T(8,128)(2,1)S(1)}, u32[]{:S(2)}, u32[]{:S(2)}) collective-permute-start(bf16[128,768]{1,0:T(8,128)(2,1)S(1)} %fusion.13), channel_id=1, source_target_pairs={{0,1},{1,0},{2,3},{3,2},{4,5},{5,4},{6,7},{7,6},{8,9},{9,8},{10,11... | collective-permute-start | bytes 589832 | tf_op jit(solution)/shard_map/ppermute | solution.py:539
  257.1 20.0 %collective-permute-start.63 = (bf16[4,48,768]{2,1,0:T(8,128)(2,1)S(1)}, bf16[4,48,768]{2,1,0:T(8,128)(2,1)S(1)}, u32[]{:S(2)}, u32[]{:S(2)}) collective-permute-start(bf16[4,48,768]{2,1,0:T(8,128)(2,1)S(1)} %fusion.2), channel_id=1, source_target_pairs={{0,1},{1,0},{2,3},{3,2},{4,5},{5,4},{6,7},{7,6},{8,9},{9,8},{10,11... | collective-permute-start | bytes 884744 | tf_op jit(solution)/shard_map/ppermute | solution.py:539
  258.4 9.8 %collective-permute-start.50 = (f32[24,768]{1,0:T(8,128)S(1)}, f32[24,768]{1,0:T(8,128)S(1)}, u32[]{:S(2)}, u32[]{:S(2)}) collective-permute-start(f32[24,768]{1,0:T(8,128)S(1)} %add.385), channel_id=1, source_target_pairs={{0,1},{1,0},{2,3},{3,2},{4,5},{5,4},{6,7},{7,6},{8,9},{9,8},{10,11... | collective-permute-start | bytes 221192 | tf_op jit(solution)/shard_map/ppermute | solution.py:539
  272.6 6.8 %collective-permute-start.54 = (f32[24,768]{1,0:T(8,128)S(1)}, f32[24,768]{1,0:T(8,128)S(1)}, u32[]{:S(2)}, u32[]{:S(2)}) collective-permute-start(f32[24,768]{1,0:T(8,128)S(1)} %add.387), channel_id=1, source_target_pairs={{0,24},{8,16},{16,8},{24,0},{1,25},{9,17},{17,9},{25,1},{2,26},{10... | collective-permute-start | bytes 221192 | tf_op jit(solution)/shard_map/ppermute | solution.py:576
  (75 other events, 400.4 us)
